TPU v7x, 32 devices: a whole 2x2x4 slice. The times are simulated.
32 devices in a mesh: mem: 4 (over y, x), lat: 8 (over z, core).
Axes of the slice: x: 2, y: 2, z: 4, core: 2. Of those that a mesh axis runs over, the one named last changes fastest.
Arguments:
- gradient: float32 [2, 4, 192, 256], P(None, 'mem', 'lat'), may hold values from -24 to 24
- perturbations: bfloat16 [16, 2, 4, 192, 256], P('mem', None, None, 'lat'), may hold values from -6 to 6
- weights: float32 [16, 4, 192, 256], P('mem', None, 'lat'), may hold values from -6 to 6
- lon_taps: float32 [25], replicated, may hold values from 0.05 to 0.3
- lat_taps: float32 [25], replicated, may hold values from 0.05 to 0.3
- lev_taps: float32 [5], replicated, may hold values from 0.2 to 0.7
- level_order: int32 [4], replicated, may hold values from 0 to 3, each once
Outputs:
- updated_weights: float32 [16, 4, 192, 256], P('mem', None, 'lat')
- increment: float32 [2, 4, 192, 256], P(None, 'mem', 'lat')
Inputs may be any that keep to these rules, and one draw needn't show every extreme that they name: `level_order`: each level appears in exactly one slot.
All inputs are finite; a program needn't handle non-finite values.
Results may differ from a plain program's by a relative error of at most 0.0003.
Values sent between devices are 32-bit elements; how exact they have to be, the bound alone decides.
A program may use at most 128 MiB of HBM per device.

v0:
```python
import functools
import math

import jax
import jax.numpy as jnp
from jax import lax
from jax.experimental import pallas as pl
from jax.experimental.pallas import tpu as pltpu
from jax.sharding import PartitionSpec as P

STEP_RATE = 0.5
TILE = 8
F32 = jnp.float32
BF16 = jnp.bfloat16


def partner(me, d, n):
    if n & (n - 1):
        return (me + d) % n
    result = 0
    bit = 1
    while bit < n:
        result = result + ((me // bit + d // bit) % 2) * bit
        bit *= 2
    return result


def split(x):
    high = x.astype(BF16)
    return high, (x - high.astype(F32)).astype(BF16)


def dot(a, b, flip=False):
    dims = (((1,), (1 if flip else 0,)), ((), ()))
    return lax.dot_general(a, b, dims, preferred_element_type=F32)


def block_of(index, size, count):
    result = jnp.zeros_like(index)
    for i in range(1, count):
        result = result + (index >= i * size).astype(jnp.int32)
    return result


def kernel(
    n, bands, norm, radius, lev_width,
    g_hbm, p_hbm, w_hbm, lon_t, lat_t, lev_t, order,
    u_ref, out_ref,
    g_all, p_ref, w_ref, x_ref, snd1, rcv1, snd2, rcv2, inc_ref, rs_ref,
    c_hi, c_lo, k1_hi, k1_lo, k2_hi, k2_lo,
    load_sem, known_sem, gs, gr, h1s, h1r, h2s, h2r, rss, rsr,
):
    me = lax.axis_index("mem")
    band = lax.axis_index("lat")
    members, _, levels, rows, lons = p_ref.shape
    own_levels = g_hbm.shape[1]
    width = 2 * radius + 1
    full = radius // TILE * TILE
    rem = radius - full
    halo = levels * radius
    fulls = levels * full
    has_low, has_high = band > 0, band < bands - 1

    load_g = pltpu.make_async_copy(g_hbm, g_all.at[0], load_sem.at[0])
    load_p = pltpu.make_async_copy(p_hbm, p_ref, load_sem.at[1])
    load_w = pltpu.make_async_copy(w_hbm, w_ref, load_sem.at[2])
    load_g.start()
    load_p.start()
    load_w.start()

    barrier = pltpu.get_barrier_semaphore()
    mesh_ids = pl.DeviceIdType.MESH
    cube = not n & (n - 1)
    direct = [d for d in range(1, n) if not cube or not d & (d - 1)]

    def greet(semaphore):
        for d in direct:
            pl.semaphore_signal(
                semaphore, inc=1, device_id=(partner(me, d, n), band), device_id_type=mesh_ids
            )

    greet(barrier)

    @pl.when(has_low)
    def _():
        pl.semaphore_signal(barrier, inc=1, device_id=(me, band - 1), device_id_type=mesh_ids)

    @pl.when(has_high)
    def _():
        pl.semaphore_signal(barrier, inc=1, device_id=(me, band + 1), device_id_type=mesh_ids)

    @pl.when(band == 0)
    def _():
        for k in range(members):
            rcv1[k, 0] = jnp.zeros((halo, lons), F32)
            rcv2[k, 0] = jnp.zeros((halo, lons), F32)

    @pl.when(band == bands - 1)
    def _():
        for k in range(members):
            rcv1[k, 1] = jnp.zeros((halo, lons), F32)
            rcv2[k, 1] = jnp.zeros((halo, lons), F32)

    load_g.wait()
    neighbours = has_low.astype(jnp.int32) + has_high.astype(jnp.int32)
    pl.semaphore_wait(barrier, len(direct) + neighbours)

    gathers = {}
    for hops in range(1, len(direct) + 1 if cube else 2):
        if hops > 1:
            greet(known_sem.at[hops - 2])
            pl.semaphore_wait(known_sem.at[hops - 2], len(direct))
        for d in range(1, n):
            if cube and bin(d).count("1") != hops:
                continue
            gathers[d] = pltpu.make_async_remote_copy(
                src_ref=g_all.at[0],
                dst_ref=g_all.at[d],
                send_sem=gs.at[d - 1],
                recv_sem=gr.at[d - 1],
                device_id=(partner(me, d, n), band),
                device_id_type=mesh_ids,
            )
            gathers[d].start()

    def source(d):
        return partner(me, d, n) if not n & (n - 1) else (me + n - d) % n

    level_of = [
        order[source(q // own_levels) * own_levels + q % own_levels] for q in range(levels)
    ]

    step = 4 * TILE

    def lon_rows(i, carry):
        first = pl.multiple_of(i * step, step)
        row = lax.broadcasted_iota(jnp.int32, (step, lons), 0) + first
        col = lax.broadcasted_iota(jnp.int32, (step, lons), 1)
        off = col - row + radius
        off = jnp.where(off < 0, off + lons, off)
        off = jnp.where(off >= lons, off - lons, off)
        value = jnp.zeros((step, lons), F32)
        for j in range(width):
            value = jnp.where(off == j, lon_t[j], value)
        high, low = split(value)
        c_hi[pl.ds(first, step), :] = high
        c_lo[pl.ds(first, step), :] = low
        return carry

    lax.fori_loop(0, lons // step, lon_rows, 0)

    total = levels * rows + 2 * halo
    row = lax.broadcasted_iota(jnp.int32, (rows, total), 0)
    col = lax.broadcasted_iota(jnp.int32, (rows, total), 1)
    in_own = col < levels * rows
    in_high = col >= levels * rows + halo
    edge = col - levels * rows - jnp.where(in_high, halo, 0)
    in_full = edge < fulls
    rest = edge - fulls
    lev_own = block_of(col, rows, levels)
    lev_full = block_of(edge, full, levels)
    lev_rest = block_of(rest, rem, levels)
    lev = jnp.where(in_own, lev_own, jnp.where(in_full, lev_full, lev_rest))
    at_full = edge - lev_full * full
    at_rest = rest - lev_rest * rem
    low_pos = jnp.where(in_full, at_full - full, at_rest - radius)
    high_pos = jnp.where(in_full, at_full + rows, at_rest + rows + full)
    pos = jnp.where(in_own, col - lev_own * rows, jnp.where(in_high, high_pos, low_pos))
    shift = pos - row
    lat_adj = jnp.zeros((rows, total), F32)
    lat_fwd = jnp.zeros((rows, total), F32)
    for j in range(width):
        lat_adj = jnp.where(shift == radius - j, lat_t[j], lat_adj)
        lat_fwd = jnp.where(shift == j - radius, lat_t[j], lat_fwd)
    coef = []
    for l in range(levels):
        coef.append([])
        for q in range(levels):
            tap = l - level_of[q] + lev_width // 2
            inside = (tap >= 0) & (tap < lev_width)
            value = lev_t[jnp.clip(tap, 0, lev_width - 1)]
            coef[l].append(jnp.where(inside, value, 0.0))
    for a in range(levels):
        adj_coef = jnp.zeros((rows, total), F32)
        fwd_coef = jnp.zeros((rows, total), F32)
        for b in range(levels):
            adj_coef = jnp.where(lev == b, coef[a][b], adj_coef)
            fwd_coef = jnp.where(lev == b, coef[b][a], fwd_coef)
        at = slice(a * rows, (a + 1) * rows)
        k1_hi[at], k1_lo[at] = split(lat_adj * adj_coef)
        k2_hi[at], k2_lo[at] = split(lat_fwd * fwd_coef)

    load_p.wait()
    load_w.wait()

    def pert(k, v, q):
        return p_ref[k, v, level_of[q]].astype(F32)

    for q in range(levels):
        d, j = divmod(q, own_levels)
        if d and not j:
            gathers[d].wait_recv()
        g0 = g_all[d, 0, j] * norm
        g1 = g_all[d, 1, j] * norm
        for k in range(members):
            x_ref[k, q * rows:(q + 1) * rows] = pert(k, 0, q) * g0 + pert(k, 1, q) * g1

    def halo_copies(snd, rcv, ss, rs, k):
        def make(side, target):
            return pltpu.make_async_remote_copy(
                src_ref=snd.at[k, side],
                dst_ref=rcv.at[k, side],
                send_sem=ss.at[k, side],
                recv_sem=rs.at[k, side],
                device_id=(me, target),
                device_id_type=mesh_ids,
            )

        return make(0, band + 1), make(1, band - 1)

    def send_halo(src, snd, rcv, ss, rs, k):
        for l in range(levels):
            base = l * rows
            snd[k, 0, l * full:(l + 1) * full] = src[k, base + rows - full:base + rows]
            snd[k, 1, l * full:(l + 1) * full] = src[k, base:base + full]
            at = slice(fulls + l * rem, fulls + (l + 1) * rem)
            snd[k, 0, at] = src[k, base + rows - radius:base + rows - full]
            snd[k, 1, at] = src[k, base + full:base + radius]
        up, down = halo_copies(snd, rcv, ss, rs, k)

        @pl.when(has_high)
        def _():
            up.start()

        @pl.when(has_low)
        def _():
            down.start()

    def wait_halo(snd, rcv, ss, rs, k):
        up, down = halo_copies(snd, rcv, ss, rs, k)

        @pl.when(has_low)
        def _():
            up.wait_recv()

        @pl.when(has_high)
        def _():
            down.wait_recv()

    def wait_sent(snd, rcv, ss, rs, k):
        up, down = halo_copies(snd, rcv, ss, rs, k)

        @pl.when(has_high)
        def _():
            up.wait_send()

        @pl.when(has_low)
        def _():
            down.wait_send()

    def apply(src, rcv, k, k_hi, k_lo, flip):
        x = jnp.concatenate([src[k], rcv[k, 0], rcv[k, 1]], axis=0)
        hi, lo = split(x)
        y = dot(k_hi[...], hi) + (dot(k_lo[...], hi) + dot(k_hi[...], lo))
        hi, lo = split(y)
        return dot(hi, c_hi[...], flip) + (dot(lo, c_hi[...], flip) + dot(hi, c_lo[...], flip))

    phase1 = (snd1, rcv1, h1s, h1r)
    phase2 = (snd2, rcv2, h2s, h2r)
    for k in range(members):
        send_halo(x_ref, *phase1, k)

    for k in range(members):
        wait_halo(*phase1, k)
        adjoint = apply(x_ref, rcv1, k, k1_hi, k1_lo, False)
        weight = w_ref[k]
        grad_total = weight + adjoint
        u_ref[k] = weight - STEP_RATE * grad_total / (1.0 + jnp.abs(grad_total))
        send_halo(u_ref, *phase2, k)

    scatters = []
    for k in range(members):
        wait_halo(*phase2, k)
        field = apply(u_ref, rcv2, k, k2_hi, k2_lo, True)
        for d in range(n - 1, -1, -1):
            for j in range(own_levels):
                q = d * own_levels + j
                part = field[q * rows:(q + 1) * rows] * norm
                for v in range(2):
                    term = pert(k, v, q) * part
                    inc_ref[d, v, j] = term if k == 0 else inc_ref[d, v, j] + term
            if d and k == members - 1:
                scatters.append(
                    pltpu.make_async_remote_copy(
                        src_ref=inc_ref.at[d],
                        dst_ref=rs_ref.at[d - 1],
                        send_sem=rss.at[d - 1],
                        recv_sem=rsr.at[d - 1],
                        device_id=(source(d), band),
                        device_id_type=mesh_ids,
                    )
                )
                scatters[-1].start()
    for k in range(members):
        wait_sent(*phase1, k)
        wait_sent(*phase2, k)
    for copy in gathers.values():
        copy.wait_send()
    for copy in scatters:
        copy.wait_recv()
    result = inc_ref[0]
    for d in range(1, n):
        result = result + rs_ref[d - 1]
    out_ref[...] = result
    for copy in scatters:
        copy.wait_send()


def write_out(u_ref, inc_ref, upd_hbm, inc_hbm, sem):
    first = pltpu.make_async_copy(u_ref, upd_hbm, sem.at[0])
    second = pltpu.make_async_copy(inc_ref, inc_hbm, sem.at[1])
    first.start()
    second.start()
    first.wait()
    second.wait()


def on_device(gradient, perturbations, weights, lon_taps, lat_taps, lev_taps, level_order):
    n, bands = lax.axis_size("mem"), lax.axis_size("lat")
    members, levels, rows, lons = weights.shape
    radius = lat_taps.shape[0] // 2
    norm = 1.0 / math.sqrt(members * n - 1)
    halo = levels * radius
    total = levels * rows + 2 * halo
    vmem, dma = pltpu.VMEM, pltpu.SemaphoreType.DMA
    anywhere = pl.BlockSpec(memory_space=pl.ANY)
    in_vmem = pl.BlockSpec(memory_space=pltpu.VMEM)
    smem = pl.BlockSpec(memory_space=pltpu.SMEM)
    updated, increment = pl.pallas_call(
        functools.partial(kernel, n, bands, norm, radius, lev_taps.shape[0]),
        out_shape=(
            vmem((members, levels * rows, lons), F32),
            vmem(gradient.shape, F32),
        ),
        in_specs=[anywhere] * 3 + [smem] * 4,
        out_specs=(in_vmem, in_vmem),
        scratch_shapes=[
            vmem((n,) + gradient.shape, F32),
            vmem(perturbations.shape, BF16),
            vmem((members, levels * rows, lons), F32),
            vmem((members, levels * rows, lons), F32),
            vmem((members, 2, halo, lons), F32),
            vmem((members, 2, halo, lons), F32),
            vmem((members, 2, halo, lons), F32),
            vmem((members, 2, halo, lons), F32),
            vmem((n,) + gradient.shape, F32),
            vmem((n - 1,) + gradient.shape, F32),
            vmem((lons, lons), BF16),
            vmem((lons, lons), BF16),
            vmem((levels * rows, total), BF16),
            vmem((levels * rows, total), BF16),
            vmem((levels * rows, total), BF16),
            vmem((levels * rows, total), BF16),
            dma((3,)),
            pltpu.SemaphoreType.REGULAR((max(1, n.bit_length() - 2),)),
            dma((n - 1,)),
            dma((n - 1,)),
            dma((members, 2)),
            dma((members, 2)),
            dma((members, 2)),
            dma((members, 2)),
            dma((n - 1,)),
            dma((n - 1,)),
        ],
        compiler_params=pltpu.CompilerParams(collective_id=0, has_side_effects=True),
        name="step",
    )(
        gradient,
        perturbations,
        weights.reshape(members, levels * rows, lons),
        lon_taps,
        lat_taps,
        lev_taps,
        level_order,
    )
    updated, increment = pl.pallas_call(
        write_out,
        out_shape=(
            jax.ShapeDtypeStruct(updated.shape, F32),
            jax.ShapeDtypeStruct(increment.shape, F32),
        ),
        in_specs=[in_vmem] * 2,
        out_specs=(anywhere, anywhere),
        scratch_shapes=[dma((2,))],
        name="write_out",
    )(
        pltpu.with_memory_space_constraint(updated, pltpu.VMEM),
        pltpu.with_memory_space_constraint(increment, pltpu.VMEM),
    )
    return updated.reshape(weights.shape), increment


def solution(mesh):
    in_specs = (
        P(None, "mem", "lat", None),
        P("mem", None, None, "lat", None),
        P("mem", None, "lat", None),
        P(),
        P(),
        P(),
        P(),
    )
    out_specs = (P("mem", None, "lat", None), P(None, "mem", "lat", None))
    return jax.shard_map(
        on_device, mesh=mesh, in_specs=in_specs, out_specs=out_specs, check_vma=False
    )
```

profile of v0, /device:TPU:0, one launch (start us, length us, event | category | flops | bytes accessed | tf_op | source)
XLA Modules:
  0.0 21.9 jit_solution(15730630058016274484)
XLA Ops:
  0.6 20.5 %step.1 = (f32[4,96,256]{2,1,0:T(8,128)S(1)}, f32[2,1,24,256]{3,2,1,0:T(8,128)S(1)}) custom-call(f32[2,1,24,256]{3,2,1,0:T(8,128)} %g_hbm.1, bf16[4,2,4,24,256]{4,3,2,1,0:T(8,128)(2,1)} %p_hbm.1, f32[4,96,256]{2,1,0:T(8,128)} %bitcast.2, f32[25]{0:T(128)} %lon_t.1, f32[25]{0:T(128)} %lat_t.1, f32[5]{0:T(128)} %lev_t.1, s32[4]{0:T(128)} %order.1), custom_call_target="tpu_custom_call" | custom-call | tf_op jit(solution)/shard_map/step/pallas_call | solution.py:339
  21.1 0.8 %write_out.1 = (f32[4,96,256]{2,1,0:T(8,128)}, f32[2,1,24,256]{3,2,1,0:T(8,128)}) custom-call(f32[4,96,256]{2,1,0:T(8,128)S(1)} %get-tuple-element.6.u_ref, f32[2,1,24,256]{3,2,1,0:T(8,128)S(1)} %get-tuple-element.7.inc_ref), custom_call_target="tpu_custom_call" | custom-call | tf_op jit(solution)/shard_map/write_out/pallas_call | solution.py:386
where the time goes:
time: 22.1 us; the launch traced here: 21.9 us
  Pallas kernels  21.3 us (96%)
  between operations  0.64 us (3%)
    pallas_call x1, Pallas kernels, on_device(): pl.pallas_call(functools.partial(kernel, n, bands, norm, radius, lev_taps...  20.5 us
    pallas_call x1, Pallas kernels, on_device(): pl.pallas_call(write_out, out_shape=(jax.ShapeDtypeStruct(updated.shape,...  0.77 us

commit v1 on v0

v1 whole, which is shorter than its diff:
```python
import functools
import math

import jax
import jax.numpy as jnp
from jax import lax
from jax.experimental import pallas as pl
from jax.experimental.pallas import tpu as pltpu
from jax.sharding import PartitionSpec as P

STEP_RATE = 0.5
TILE = 8
PACK = 16
F32 = jnp.float32
BF16 = jnp.bfloat16


def partner(me, d, n):
    if n & (n - 1):
        return (me + d) % n
    result = 0
    bit = 1
    while bit < n:
        result = result + ((me // bit + d // bit) % 2) * bit
        bit *= 2
    return result


def split(x):
    high = x.astype(BF16)
    return high, (x - high.astype(F32)).astype(BF16)


def dot(a, b):
    return lax.dot_general(a, b, (((1,), (0,)), ((), ())), preferred_element_type=F32)


def filter_lon(x, c_hi, c_lo):
    high, low = split(x)
    return dot(high, c_hi[...]) + (dot(low, c_hi[...]) + dot(high, c_lo[...]))


def stacked(x):
    high, low = split(x)
    return jnp.concatenate([high, high, low], axis=0)


def iota(shape, axis):
    return lax.broadcasted_iota(jnp.int32, shape, axis)


def sizes(rows, radius):
    full = radius // TILE * TILE
    rem = radius - full
    if 2 * rem > TILE or 2 * radius > rows:
        raise NotImplementedError("radius")
    halo = 2 * full + (TILE if rem else 0)
    edge = full + (TILE if rem else 0)
    deep = -(-3 * rows // PACK) * PACK
    wide = -(-(rows + halo) // PACK) * PACK
    return full, rem, halo, edge, deep, wide


def kernel(
    n, bands, norm, radius, lev_width,
    g_hbm, p_hbm, w_hbm, lon_hbm, lat_hbm, lev_hbm, order_hbm,
    u_ref, out_ref,
    g_all, p_ref, pf_ref, w_ref, wn_ref, wh_ref, z_ref, zn_ref, acc_ref, f_ref, inc_ref, rs_ref,
    a_hi, a_lo, b_hi, b_lo, k1, k2,
    lon_t, lat_t, lev_t, order,
    load_sem, known_sem, gs, gr, zs, zr, ws, wr, rss, rsr,
):
    me = lax.axis_index("mem")
    band = lax.axis_index("lat")
    members, _, levels, rows, lons = p_ref.shape
    own_levels = g_hbm.shape[1]
    width = 2 * radius + 1
    full, rem, halo, edge, deep, wide = sizes(rows, radius)
    stack = members * rows
    has_low, has_high = band > 0, band < bands - 1
    mesh_ids = pl.DeviceIdType.MESH

    loads = [
        pltpu.make_async_copy(src, dst, load_sem.at[i])
        for i, (src, dst) in enumerate([
            (g_hbm, g_all.at[0]), (lon_hbm, lon_t), (lat_hbm, lat_t), (lev_hbm, lev_t),
            (order_hbm, order), (p_hbm, p_ref), (w_hbm, w_ref),
        ])
    ]
    load_g, load_lon, load_lat, load_lev, load_order, load_p, load_w = loads
    for copy in loads:
        copy.start()

    barrier = pltpu.get_barrier_semaphore()
    cube = not n & (n - 1)
    direct = [d for d in range(1, n) if not cube or not d & (d - 1)]
    rounds = [[d for d in range(1, n) if not cube or bin(d).count("1") == hops]
              for hops in range(1, len(direct) + 1 if cube else 2)]
    arrival = [0] + [d for ds in rounds for d in ds]

    def greet(semaphore):
        for d in direct:
            pl.semaphore_signal(
                semaphore, inc=1, device_id=(partner(me, d, n), band), device_id_type=mesh_ids
            )

    greet(barrier)

    @pl.when(has_low)
    def _():
        pl.semaphore_signal(barrier, inc=1, device_id=(me, band - 1), device_id_type=mesh_ids)

    @pl.when(has_high)
    def _():
        pl.semaphore_signal(barrier, inc=1, device_id=(me, band + 1), device_id_type=mesh_ids)

    for side, present in ((0, has_low), (1, has_high)):
        @pl.when(jnp.logical_not(present))
        def _():
            for q in range(levels):
                zn_ref[side, q] = jnp.zeros((stack, lons), F32)
            wn_ref[side] = jnp.zeros(wn_ref.shape[1:], F32)

    load_lon.wait()
    row, col = iota((TILE, lons), 0), iota((TILE, lons), 1)
    for c_hi, c_lo, sign in ((a_hi, a_lo, 1), (b_hi, b_lo, -1)):
        off = sign * (col - row) + radius
        off = jnp.where(off < 0, off + lons, off)
        off = jnp.where(off >= lons, off - lons, off)
        base = jnp.zeros((TILE, lons), F32)
        for j in range(width):
            base = jnp.where(off == j, lon_t[j], base)
        for i in range(0, lons, PACK):
            value = jnp.concatenate(
                [pltpu.roll(base, i, 1) if i else base, pltpu.roll(base, i + TILE, 1)], axis=0
            )
            c_hi[i:i + PACK], c_lo[i:i + PACK] = split(value)

    load_lat.wait()

    def thirds(c, size):
        third = (c >= size).astype(jnp.int32) + (c >= 2 * size).astype(jnp.int32)
        return third, c - third * size

    def halo_pos(h):
        s = h - 2 * full
        rest = jnp.where(s < rem, rows + full + s, s - full - TILE)
        rest = jnp.where((s >= rem) & (s < TILE - rem), -4 * rows, rest)
        return jnp.where(h < full, h - full, jnp.where(h < 2 * full, rows + h - full, rest))

    def lat_matrix(out_pos, in_pos, third, sign):
        shift = sign * (in_pos - out_pos)
        value = jnp.zeros(shift.shape, F32)
        for j in range(width):
            value = jnp.where(shift == j - radius, lat_t[j], value)
        high = value.astype(BF16).astype(F32)
        return jnp.where(third == 1, value - high, high).astype(BF16)

    r = iota(k1.shape, 0)
    third, c = thirds(iota(k1.shape, 1), deep)
    out_pos = jnp.where(r < rows, r, halo_pos(r - rows))
    in_pos = jnp.where(c < rows, c, jnp.where(c < 2 * rows, c - 2 * rows, c - rows))
    in_pos = jnp.where(c < 3 * rows, in_pos, 8 * rows)
    k1[...] = lat_matrix(out_pos, in_pos, third, -1)
    r = iota(k2.shape, 0)
    third, c = thirds(iota(k2.shape, 1), wide)
    in_pos = jnp.where(c < rows, c, halo_pos(c - rows))
    in_pos = jnp.where(c < rows + halo, in_pos, 8 * rows)
    inside = (in_pos + band * rows >= 0) & (in_pos + band * rows < bands * rows)
    k2[...] = lat_matrix(r, jnp.where(inside, in_pos, 8 * rows), third, 1)

    def source(d):
        return partner(me, d, n) if cube else (me + n - d) % n

    load_lev.wait()
    load_order.wait()
    level_of = [
        order[source(q // own_levels) * own_levels + q % own_levels] for q in range(levels)
    ]
    coef = []
    for l in range(levels):
        coef.append([])
        for q in range(levels):
            tap = l - level_of[q] + lev_width // 2
            inside = (tap >= 0) & (tap < lev_width)
            value = lev_t[jnp.clip(tap, 0, lev_width - 1)]
            coef[l].append(jnp.where(inside, value, 0.0))

    load_p.wait()
    for q in range(levels):
        for v in range(2):
            for k in range(members):
                pf_ref[q, v, k * rows:(k + 1) * rows] = p_ref[k, v, level_of[q]].astype(F32) * norm
    load_w.wait()
    load_g.wait()

    gathers = {
        d: pltpu.make_async_remote_copy(
            src_ref=g_all.at[0],
            dst_ref=g_all.at[d],
            send_sem=gs.at[d - 1],
            recv_sem=gr.at[d - 1],
            device_id=(partner(me, d, n), band),
            device_id_type=mesh_ids,
        )
        for d in range(1, n)
    }

    def to_bands(low_src, high_src, dst, send_sem, recv_sem):
        def make(side, src, target):
            return pltpu.make_async_remote_copy(
                src_ref=src,
                dst_ref=dst(side),
                send_sem=send_sem(side),
                recv_sem=recv_sem(side),
                device_id=(me, target),
                device_id_type=mesh_ids,
            )

        return make(0, low_src, band + 1), make(1, high_src, band - 1)

    def start(copies):
        pl.when(has_high)(copies[0].start)
        pl.when(has_low)(copies[1].start)

    def wait_recv(copies):
        pl.when(has_low)(copies[0].wait_recv)
        pl.when(has_high)(copies[1].wait_recv)

    def wait_send(copies):
        pl.when(has_high)(copies[0].wait_send)
        pl.when(has_low)(copies[1].wait_send)

    w_copies = to_bands(
        w_ref.at[:, :, rows - edge:rows, :], w_ref.at[:, :, 0:edge, :],
        lambda s: wn_ref.at[s], lambda s: ws.at[s], lambda s: wr.at[s],
    )
    z_copies = [
        to_bands(
            z_ref.at[q], z_ref.at[q],
            lambda s, q=q: zn_ref.at[s, q], lambda s, q=q: zs.at[s, q], lambda s, q=q: zr.at[s, q],
        )
        for q in range(levels)
    ]

    neighbours = has_low.astype(jnp.int32) + has_high.astype(jnp.int32)
    pl.semaphore_wait(barrier, len(direct) + neighbours)
    if len(rounds) > 1:
        greet(known_sem.at[0])
    for d in rounds[0]:
        gathers[d].start()
    start(w_copies)

    def send_level(q):
        d, j = divmod(q, own_levels)
        g0 = jnp.concatenate([g_all[d, 0, j]] * members, axis=0)
        g1 = jnp.concatenate([g_all[d, 1, j]] * members, axis=0)
        z_ref[q] = filter_lon(pf_ref[q, 0] * g0 + pf_ref[q, 1] * g1, a_hi, a_lo)
        start(z_copies[q])

    for j in range(own_levels):
        send_level(j)
    for i in range(1, len(rounds)):
        pl.semaphore_wait(known_sem.at[i - 1], len(direct))
        if i + 1 < len(rounds):
            greet(known_sem.at[i])
        for d in rounds[i]:
            gathers[d].start()
    for d in arrival[1:]:
        gathers[d].wait_recv()
        for j in range(own_levels):
            send_level(d * own_levels + j)

    wait_recv(w_copies)
    s = iota((TILE, lons), 0)
    for k in range(members):
        for l in range(levels):
            wh_ref[k, l, 0:full] = wn_ref[0, k, l, edge - full:edge]
            wh_ref[k, l, full:2 * full] = wn_ref[1, k, l, 0:full]
            if rem:
                wh_ref[k, l, 2 * full:halo] = jnp.where(
                    s < rem, wn_ref[1, k, l, full:edge], wn_ref[0, k, l, 0:TILE]
                )

    ordered = [d * own_levels + j for d in arrival for j in range(own_levels)]
    gap = jnp.zeros((deep - 3 * rows, lons), F32)
    for step, q in enumerate(ordered):
        wait_recv(z_copies[q])
        for k in range(members):
            at = slice(k * rows, (k + 1) * rows)
            x = jnp.concatenate([z_ref[q, at], zn_ref[0, q, at], zn_ref[1, q, at], gap], axis=0)
            y = dot(k1[...], stacked(x))
            if step < levels - 1:
                for l in range(levels):
                    if step:
                        acc_ref[k, l] = acc_ref[k, l] + coef[l][q] * y
                    else:
                        w = jnp.concatenate([w_ref[k, l], wh_ref[k, l]], axis=0)
                        acc_ref[k, l] = w + coef[l][q] * y
                continue
            parts = []
            for l in range(levels):
                w = jnp.concatenate([w_ref[k, l], wh_ref[k, l]], axis=0)
                total = acc_ref[k, l] + coef[l][q] * y
                u = w - STEP_RATE * total / (1.0 + jnp.abs(total))
                u_ref[k, l] = u[0:rows]
                if wide > rows + halo:
                    u = jnp.concatenate([u, jnp.zeros((wide - rows - halo, lons), F32)], axis=0)
                parts.append(dot(k2[...], stacked(u)))
            f_ref[k] = filter_lon(jnp.concatenate(parts, axis=0), b_hi, b_lo)

    scatters = []
    for d in reversed(arrival):
        for j in range(own_levels):
            q = d * own_levels + j
            inc = [jnp.zeros((rows, lons), F32)] * 2
            for k in range(members):
                field = coef[0][q] * f_ref[k, 0:rows]
                for l in range(1, levels):
                    field = field + coef[l][q] * f_ref[k, l * rows:(l + 1) * rows]
                for v in range(2):
                    inc[v] = inc[v] + pf_ref[q, v, k * rows:(k + 1) * rows] * field
            for v in range(2):
                inc_ref[d, v, j] = inc[v]
        if d:
            scatters.append(
                pltpu.make_async_remote_copy(
                    src_ref=inc_ref.at[d],
                    dst_ref=rs_ref.at[d - 1],
                    send_sem=rss.at[d - 1],
                    recv_sem=rsr.at[d - 1],
                    device_id=(source(d), band),
                    device_id_type=mesh_ids,
                )
            )
            scatters[-1].start()
    wait_send(w_copies)
    for copies in z_copies:
        wait_send(copies)
    for copy in gathers.values():
        copy.wait_send()
    result = inc_ref[0]
    for copy, d in zip(scatters, [d for d in reversed(arrival) if d]):
        copy.wait_recv()
        result = result + rs_ref[d - 1]
    out_ref[...] = result
    for copy in scatters:
        copy.wait_send()


def write_out(u_ref, inc_ref, upd_hbm, inc_hbm, sem):
    first = pltpu.make_async_copy(u_ref, upd_hbm, sem.at[0])
    second = pltpu.make_async_copy(inc_ref, inc_hbm, sem.at[1])
    first.start()
    second.start()
    first.wait()
    second.wait()


def on_device(gradient, perturbations, weights, lon_taps, lat_taps, lev_taps, level_order):
    n, bands = lax.axis_size("mem"), lax.axis_size("lat")
    members, levels, rows, lons = weights.shape
    radius = lat_taps.shape[0] // 2
    norm = 1.0 / math.sqrt(members * n - 1)
    full, rem, halo, edge, deep, wide = sizes(rows, radius)
    stack = members * rows
    vmem, dma = pltpu.VMEM, pltpu.SemaphoreType.DMA
    anywhere = pl.BlockSpec(memory_space=pl.ANY)
    in_vmem = pl.BlockSpec(memory_space=pltpu.VMEM)
    updated, increment = pl.pallas_call(
        functools.partial(kernel, n, bands, norm, radius, lev_taps.shape[0]),
        out_shape=(
            vmem(weights.shape, F32),
            vmem(gradient.shape, F32),
        ),
        in_specs=[anywhere] * 7,
        out_specs=(in_vmem, in_vmem),
        scratch_shapes=[
            vmem((n,) + gradient.shape, F32),
            vmem(perturbations.shape, BF16),
            vmem((levels, 2, stack, lons), F32),
            vmem(weights.shape, F32),
            vmem((2, members, levels, edge, lons), F32),
            vmem((members, levels, halo, lons), F32),
            vmem((levels, stack, lons), F32),
            vmem((2, levels, stack, lons), F32),
            vmem((members, levels, rows + halo, lons), F32),
            vmem((members, levels * rows, lons), F32),
            vmem((n,) + gradient.shape, F32),
            vmem((n - 1,) + gradient.shape, F32),
            vmem((lons, lons), BF16),
            vmem((lons, lons), BF16),
            vmem((lons, lons), BF16),
            vmem((lons, lons), BF16),
            vmem((rows + halo, 3 * deep), BF16),
            vmem((rows, 3 * wide), BF16),
            pltpu.SMEM(lon_taps.shape, F32),
            pltpu.SMEM(lat_taps.shape, F32),
            pltpu.SMEM(lev_taps.shape, F32),
            pltpu.SMEM(level_order.shape, jnp.int32),
            dma((7,)),
            pltpu.SemaphoreType.REGULAR((max(1, n.bit_length() - 2),)),
            dma((n - 1,)),
            dma((n - 1,)),
            dma((2, levels)),
            dma((2, levels)),
            dma((2,)),
            dma((2,)),
            dma((n - 1,)),
            dma((n - 1,)),
        ],
        compiler_params=pltpu.CompilerParams(collective_id=0, has_side_effects=True),
        name="step",
    )(gradient, perturbations, weights, lon_taps, lat_taps, lev_taps, level_order)
    return pl.pallas_call(
        write_out,
        out_shape=(
            jax.ShapeDtypeStruct(updated.shape, F32),
            jax.ShapeDtypeStruct(increment.shape, F32),
        ),
        in_specs=[in_vmem] * 2,
        out_specs=(anywhere, anywhere),
        scratch_shapes=[dma((2,))],
        name="write_out",
    )(
        pltpu.with_memory_space_constraint(updated, pltpu.VMEM),
        pltpu.with_memory_space_constraint(increment, pltpu.VMEM),
    )


def solution(mesh):
    in_specs = (
        P(None, "mem", "lat", None),
        P("mem", None, None, "lat", None),
        P("mem", None, "lat", None),
        P(),
        P(),
        P(),
        P(),
    )
    out_specs = (P("mem", None, "lat", None), P(None, "mem", "lat", None))
    return jax.shard_map(
        on_device, mesh=mesh, in_specs=in_specs, out_specs=out_specs, check_vma=False
    )
```

time: 22.1 us -> 19.5 us (0.88)
  the two profiles are of different devices: /device:TPU:0 before, /device:TPU:1 now
where the time goes in v1:
time: 19.5 us; the launch traced here: 19.4 us
  Pallas kernels  18.7 us (96%)
  between operations  0.64 us (3%)
    pallas_call x1, Pallas kernels, on_device(): pl.pallas_call(functools.partial(kernel, n, bands, norm, radius, lev_taps...  17.9 us
    pallas_call x1, Pallas kernels, on_device(): pl.pallas_call(write_out, out_shape=(jax.ShapeDtypeStruct(updated.shape,...  0.77 us

profile of v1, /device:TPU:1, one launch (start us, length us, event | category | flops | bytes accessed | tf_op | source)
XLA Modules:
  0.0 19.4 jit_solution(2409377704864791504)
XLA Ops:
  0.6 17.9 %step.1 = (f32[4,4,24,256]{3,2,1,0:T(8,128)S(1)}, f32[2,1,24,256]{3,2,1,0:T(8,128)S(1)}) custom-call(f32[2,1,24,256]{3,2,1,0:T(8,128)} %g_hbm.1, bf16[4,2,4,24,256]{4,3,2,1,0:T(8,128)(2,1)} %p_hbm.1, f32[4,4,24,256]{3,2,1,0:T(8,128)} %w_hbm.1, f32[25]{0:T(128)} %lon_hbm.1, f32[25]{0:T(128)} %lat_hbm.1, f32[5]{0:T(128)} %lev_hbm.1, s32[4]{0:T(128)} %order_hbm.1), custom_call_target="tpu_custom_call" | custom-call | tf_op jit(solution)/shard_map/step/pallas_call | solution.py:370
  18.6 0.8 %write_out.1 = (f32[4,4,24,256]{3,2,1,0:T(8,128)}, f32[2,1,24,256]{3,2,1,0:T(8,128)}) custom-call(f32[4,4,24,256]{3,2,1,0:T(8,128)S(1)} %get-tuple-element.4.u_ref, f32[2,1,24,256]{3,2,1,0:T(8,128)S(1)} %get-tuple-element.5.inc_ref), custom_call_target="tpu_custom_call" | custom-call | tf_op jit(solution)/shard_map/write_out/pallas_call | solution.py:415

commit v2 on v1

v2 whole, which is shorter than its diff:
```python
import functools
import math

import jax
import jax.numpy as jnp
from jax import lax
from jax.experimental import pallas as pl
from jax.experimental.pallas import tpu as pltpu
from jax.sharding import PartitionSpec as P

STEP_RATE = 0.5
TILE = 8
PACK = 16
F32 = jnp.float32
BF16 = jnp.bfloat16


def partner(me, d, n):
    if n & (n - 1):
        return (me + d) % n
    result = 0
    bit = 1
    while bit < n:
        result = result + ((me // bit + d // bit) % 2) * bit
        bit *= 2
    return result


def split(x):
    high = x.astype(BF16)
    return high, (x - high.astype(F32)).astype(BF16)


def dot(a, b):
    return lax.dot_general(a, b, (((1,), (0,)), ((), ())), preferred_element_type=F32)


def filter_lon(x, c_hi, c_lo):
    high, low = split(x)
    both = dot(jnp.concatenate([high, low], axis=0), c_hi[...])
    return both[:x.shape[0]] + (both[x.shape[0]:] + dot(high, c_lo[...]))


def packed(rows):
    return -(-rows // PACK) * PACK


def stacked(x):
    pad = packed(x.shape[0]) - x.shape[0]
    if pad:
        x = jnp.concatenate([x, jnp.zeros((pad, x.shape[1]), F32)], axis=0)
    high, low = split(x)
    return jnp.concatenate([high, high, low], axis=0)


def iota(shape, axis):
    return lax.broadcasted_iota(jnp.int32, shape, axis)


def sizes(rows, radius):
    full = radius // TILE * TILE
    rem = radius - full
    if 2 * rem > TILE or 2 * radius > rows:
        raise NotImplementedError("radius")
    halo = 2 * full + (TILE if rem else 0)
    edge = full + (TILE if rem else 0)
    return full, rem, halo, edge


def kernel(
    n, bands, norm, radius, lev_width,
    g_hbm, p_hbm, w_hbm, lon_hbm, lat_hbm, lev_hbm, order_hbm,
    u_ref, out_ref,
    g_all, p_ref, pf_ref, w_ref, wn_ref, wh_ref, z_ref, zn_ref, acc_ref, f_ref, inc_ref, rs_ref,
    a_hi, a_lo, b_hi, b_lo, k_own, k_halo, k_fwd,
    lon_t, lat_t, lev_t, order,
    load_sem, known_sem, gs, gr, zs, zr, ws, wr, rsr,
):
    me = lax.axis_index("mem")
    band = lax.axis_index("lat")
    members, _, levels, rows, lons = p_ref.shape
    own_levels = g_hbm.shape[1]
    width = 2 * radius + 1
    full, rem, halo, edge = sizes(rows, radius)
    stack = members * rows
    has_low, has_high = band > 0, band < bands - 1
    mesh_ids = pl.DeviceIdType.MESH

    loads = [
        pltpu.make_async_copy(src, dst, load_sem.at[i])
        for i, (src, dst) in enumerate([
            (g_hbm, g_all.at[0]), (w_hbm, w_ref), (lon_hbm, lon_t), (order_hbm, order),
            (p_hbm, p_ref), (lev_hbm, lev_t), (lat_hbm, lat_t),
        ])
    ]
    load_g, load_w, load_lon, load_order, load_p, load_lev, load_lat = loads
    for copy in loads:
        copy.start()

    barrier = pltpu.get_barrier_semaphore()
    cube = not n & (n - 1)
    direct = [d for d in range(1, n) if not cube or not d & (d - 1)]
    rounds = [[d for d in range(1, n) if not cube or bin(d).count("1") == hops]
              for hops in range(1, len(direct) + 1 if cube else 2)]
    arrival = [0] + [d for ds in rounds for d in ds]

    def greet(semaphore):
        for d in direct:
            pl.semaphore_signal(
                semaphore, inc=1, device_id=(partner(me, d, n), band), device_id_type=mesh_ids
            )

    greet(barrier)

    @pl.when(has_low)
    def _():
        pl.semaphore_signal(barrier, inc=1, device_id=(me, band - 1), device_id_type=mesh_ids)

    @pl.when(has_high)
    def _():
        pl.semaphore_signal(barrier, inc=1, device_id=(me, band + 1), device_id_type=mesh_ids)

    def source(d):
        return partner(me, d, n) if cube else (me + n - d) % n

    gathers = {
        d: pltpu.make_async_remote_copy(
            src_ref=g_all.at[0],
            dst_ref=g_all.at[d],
            send_sem=gs.at[d - 1],
            recv_sem=gr.at[d - 1],
            device_id=(partner(me, d, n), band),
            device_id_type=mesh_ids,
        )
        for d in range(1, n)
    }

    def to_bands(low_src, high_src, dst, send_sem, recv_sem):
        def make(side, src, target):
            return pltpu.make_async_remote_copy(
                src_ref=src,
                dst_ref=dst(side),
                send_sem=send_sem(side),
                recv_sem=recv_sem(side),
                device_id=(me, target),
                device_id_type=mesh_ids,
            )

        return make(0, low_src, band + 1), make(1, high_src, band - 1)

    def start(copies):
        pl.when(has_high)(copies[0].start)
        pl.when(has_low)(copies[1].start)

    def wait_recv(copies):
        pl.when(has_low)(copies[0].wait_recv)
        pl.when(has_high)(copies[1].wait_recv)

    def wait_send(copies):
        pl.when(has_high)(copies[0].wait_send)
        pl.when(has_low)(copies[1].wait_send)

    def w_copy(i, size, low, high):
        at = low - rows + edge, high
        return to_bands(
            w_ref.at[:, :, low:low + size, :], w_ref.at[:, :, high:high + size, :],
            lambda s: wn_ref.at[s, :, :, at[s]:at[s] + size, :],
            lambda s: ws.at[s, i], lambda s: wr.at[s, i],
        )

    w_copies = [w_copy(0, full, rows - full, 0)]
    if rem:
        w_copies.append(w_copy(1, rem, rows - radius, full))
    z_copies = [
        to_bands(
            z_ref.at[q], z_ref.at[q],
            lambda s, q=q: zn_ref.at[s, q], lambda s, q=q: zs.at[s, q], lambda s, q=q: zr.at[s, q],
        )
        for q in range(levels)
    ]

    load_g.wait()
    neighbours = has_low.astype(jnp.int32) + has_high.astype(jnp.int32)
    pl.semaphore_wait(barrier, len(direct) + neighbours)
    if len(rounds) > 1:
        greet(known_sem.at[0])
    for d in rounds[0]:
        gathers[d].start()
    load_w.wait()
    for copies in w_copies:
        start(copies)

    row, col = iota((TILE, lons), 0), iota((TILE, lons), 1)

    def lon_matrix(c_hi, c_lo, sign):
        off = sign * (col - row) + radius
        off = jnp.where(off < 0, off + lons, off)
        off = jnp.where(off >= lons, off - lons, off)
        base = jnp.zeros((TILE, lons), F32)
        for j in range(width):
            base = jnp.where(off == j, lon_t[j], base)
        for i in range(0, lons, PACK):
            value = jnp.concatenate(
                [pltpu.roll(base, i, 1) if i else base, pltpu.roll(base, i + TILE, 1)], axis=0
            )
            c_hi[i:i + PACK], c_lo[i:i + PACK] = split(value)

    load_lon.wait()
    lon_matrix(a_hi, a_lo, 1)
    load_order.wait()
    level_of = [
        order[source(q // own_levels) * own_levels + q % own_levels] for q in range(levels)
    ]
    load_p.wait()

    def scaled(q):
        for v in range(2):
            for k in range(members):
                pf_ref[q, v, k * rows:(k + 1) * rows] = p_ref[k, v, level_of[q]].astype(F32) * norm

    def send_level(q):
        d, j = divmod(q, own_levels)
        g0 = jnp.concatenate([g_all[d, 0, j]] * members, axis=0)
        g1 = jnp.concatenate([g_all[d, 1, j]] * members, axis=0)
        z_ref[q] = filter_lon(pf_ref[q, 0] * g0 + pf_ref[q, 1] * g1, a_hi, a_lo)
        start(z_copies[q])

    for j in range(own_levels):
        scaled(j)
        send_level(j)
    for i in range(1, len(rounds)):
        pl.semaphore_wait(known_sem.at[i - 1], len(direct))
        if i + 1 < len(rounds):
            greet(known_sem.at[i])
        for d in rounds[i]:
            gathers[d].start()

    for q in range(own_levels, levels):
        scaled(q)
    for side, present in ((0, has_low), (1, has_high)):
        @pl.when(jnp.logical_not(present))
        def _():
            for q in range(levels):
                zn_ref[side, q] = jnp.zeros((stack, lons), F32)
            wn_ref[side] = jnp.zeros(wn_ref.shape[1:], F32)

    lon_matrix(b_hi, b_lo, -1)
    load_lat.wait()

    def thirds(shape):
        c, size = iota(shape, 1), shape[1] // 3
        third = (c >= size).astype(jnp.int32) + (c >= 2 * size).astype(jnp.int32)
        return third, c - third * size

    def halo_pos(h):
        s = h - 2 * full
        rest = jnp.where(s < rem, rows + full + s, s - full - TILE)
        rest = jnp.where((s >= rem) & (s < TILE - rem), -4 * rows, rest)
        return jnp.where(h < full, h - full, jnp.where(h < 2 * full, rows + h - full, rest))

    def lat_matrix(out_pos, in_pos, third, sign):
        shift = sign * (in_pos - out_pos)
        value = jnp.zeros(shift.shape, F32)
        for j in range(width):
            value = jnp.where(shift == j - radius, lat_t[j], value)
        high = value.astype(BF16).astype(F32)
        return jnp.where(third == 1, value - high, high).astype(BF16)

    far = 8 * rows
    for k_ref, is_own in ((k_own, True), (k_halo, False)):
        r = iota(k_ref.shape, 0)
        third, c = thirds(k_ref.shape)
        if is_own:
            in_pos = jnp.where(c < rows, c, far)
        else:
            in_pos = jnp.where(c < rows, c - rows, jnp.where(c < 2 * rows, c, far))
        out_pos = jnp.where(r < rows, r, halo_pos(r - rows))
        k_ref[...] = lat_matrix(out_pos, in_pos, third, -1)
    third, c = thirds(k_fwd.shape)
    in_pos = jnp.where(c < rows, c, halo_pos(c - rows))
    inside = (in_pos + band * rows >= 0) & (in_pos + band * rows < bands * rows)
    inside = inside & (c < rows + halo)
    k_fwd[...] = lat_matrix(iota(k_fwd.shape, 0), jnp.where(inside, in_pos, far), third, 1)

    load_lev.wait()
    coef = []
    for l in range(levels):
        coef.append([])
        for q in range(levels):
            tap = l - level_of[q] + lev_width // 2
            inside = (tap >= 0) & (tap < lev_width)
            value = lev_t[jnp.clip(tap, 0, lev_width - 1)]
            coef[l].append(jnp.where(inside, value, 0.0))

    for d in arrival[1:]:
        gathers[d].wait_recv()
        for j in range(own_levels):
            send_level(d * own_levels + j)

    for copies in w_copies:
        wait_recv(copies)
    s = iota((TILE, lons), 0)
    for k in range(members):
        at = slice(k * rows, (k + 1) * rows)
        for l in range(levels):
            wh_ref[k, l, 0:full] = wn_ref[0, k, l, edge - full:edge]
            wh_ref[k, l, full:2 * full] = wn_ref[1, k, l, 0:full]
            if rem:
                wh_ref[k, l, 2 * full:halo] = jnp.where(
                    s < rem, wn_ref[1, k, l, full:edge], wn_ref[0, k, l, 0:TILE]
                )
        own = [dot(k_own[...], stacked(z_ref[q, at])) for q in range(levels)]
        for l in range(levels):
            total = jnp.concatenate([w_ref[k, l], wh_ref[k, l]], axis=0)
            for q in range(levels):
                total = total + coef[l][q] * own[q]
            acc_ref[k, l] = total
    for copies in w_copies:
        wait_send(copies)
    for copy in gathers.values():
        copy.wait_send()

    ordered = [d * own_levels + j for d in arrival for j in range(own_levels)]
    for q in ordered[:-1]:
        wait_recv(z_copies[q])
        for k in range(members):
            at = slice(k * rows, (k + 1) * rows)
            y = dot(k_halo[...], stacked(jnp.concatenate([zn_ref[0, q, at], zn_ref[1, q, at]], axis=0)))
            for l in range(levels):
                acc_ref[k, l] = acc_ref[k, l] + coef[l][q] * y
        wait_send(z_copies[q])

    q = ordered[-1]
    wait_recv(z_copies[q])
    for k in range(members):
        at = slice(k * rows, (k + 1) * rows)
        y = dot(k_halo[...], stacked(jnp.concatenate([zn_ref[0, q, at], zn_ref[1, q, at]], axis=0)))
        for l in range(levels):
            w = jnp.concatenate([w_ref[k, l], wh_ref[k, l]], axis=0)
            total = acc_ref[k, l] + coef[l][q] * y
            u = w - STEP_RATE * total / (1.0 + jnp.abs(total))
            u_ref[k, l] = u[0:rows]
            f_ref[k, l] = dot(k_fwd[...], stacked(u))

    fields = []
    for d in reversed(arrival):
        for j in range(own_levels):
            for k in range(members):
                field = coef[0][d * own_levels + j] * f_ref[k, 0]
                for l in range(1, levels):
                    field = field + coef[l][d * own_levels + j] * f_ref[k, l]
                fields.append(field)
    fields = filter_lon(jnp.concatenate(fields, axis=0), b_hi, b_lo)

    scatters = []
    for i, d in enumerate(reversed(arrival)):
        for j in range(own_levels):
            q = d * own_levels + j
            at = (i * own_levels + j) * stack
            for v in range(2):
                terms = pf_ref[q, v] * fields[at:at + stack]
                inc = terms[0:rows]
                for k in range(1, members):
                    inc = inc + terms[k * rows:(k + 1) * rows]
                inc_ref[d, v, j] = inc
        if d:
            scatters.append(
                pltpu.make_async_remote_copy(
                    src_ref=inc_ref.at[d],
                    dst_ref=rs_ref.at[d - 1],
                    send_sem=gs.at[d - 1],
                    recv_sem=rsr.at[d - 1],
                    device_id=(source(d), band),
                    device_id_type=mesh_ids,
                )
            )
            scatters[-1].start()
    wait_send(z_copies[ordered[-1]])
    result = inc_ref[0]
    for copy, d in zip(scatters, [d for d in reversed(arrival) if d]):
        copy.wait_recv()
        result = result + rs_ref[d - 1]
    out_ref[...] = result
    for copy in scatters:
        copy.wait_send()


def write_out(u_ref, inc_ref, upd_hbm, inc_hbm, sem):
    first = pltpu.make_async_copy(u_ref, upd_hbm, sem.at[0])
    second = pltpu.make_async_copy(inc_ref, inc_hbm, sem.at[1])
    first.start()
    second.start()
    first.wait()
    second.wait()


def on_device(gradient, perturbations, weights, lon_taps, lat_taps, lev_taps, level_order):
    n, bands = lax.axis_size("mem"), lax.axis_size("lat")
    members, levels, rows, lons = weights.shape
    radius = lat_taps.shape[0] // 2
    norm = 1.0 / math.sqrt(members * n - 1)
    full, rem, halo, edge = sizes(rows, radius)
    stack = members * rows
    vmem, dma = pltpu.VMEM, pltpu.SemaphoreType.DMA
    anywhere = pl.BlockSpec(memory_space=pl.ANY)
    in_vmem = pl.BlockSpec(memory_space=pltpu.VMEM)
    updated, increment = pl.pallas_call(
        functools.partial(kernel, n, bands, norm, radius, lev_taps.shape[0]),
        out_shape=(
            vmem(weights.shape, F32),
            vmem(gradient.shape, F32),
        ),
        in_specs=[anywhere] * 7,
        out_specs=(in_vmem, in_vmem),
        scratch_shapes=[
            vmem((n,) + gradient.shape, F32),
            vmem(perturbations.shape, BF16),
            vmem((levels, 2, stack, lons), F32),
            vmem(weights.shape, F32),
            vmem((2, members, levels, edge, lons), F32),
            vmem((members, levels, halo, lons), F32),
            vmem((levels, stack, lons), F32),
            vmem((2, levels, stack, lons), F32),
            vmem((members, levels, rows + halo, lons), F32),
            vmem(weights.shape, F32),
            vmem((n,) + gradient.shape, F32),
            vmem((n - 1,) + gradient.shape, F32),
            vmem((lons, lons), BF16),
            vmem((lons, lons), BF16),
            vmem((lons, lons), BF16),
            vmem((lons, lons), BF16),
            vmem((rows + halo, 3 * packed(rows)), BF16),
            vmem((rows + halo, 3 * packed(2 * rows)), BF16),
            vmem((rows, 3 * packed(rows + halo)), BF16),
            pltpu.SMEM(lon_taps.shape, F32),
            pltpu.SMEM(lat_taps.shape, F32),
            pltpu.SMEM(lev_taps.shape, F32),
            pltpu.SMEM(level_order.shape, jnp.int32),
            dma((7,)),
            pltpu.SemaphoreType.REGULAR((max(1, n.bit_length() - 2),)),
            dma((n - 1,)),
            dma((n - 1,)),
            dma((2, levels)),
            dma((2, levels)),
            dma((2, 2)),
            dma((2, 2)),
            dma((n - 1,)),
        ],
        compiler_params=pltpu.CompilerParams(collective_id=0, has_side_effects=True),
        name="step",
    )(gradient, perturbations, weights, lon_taps, lat_taps, lev_taps, level_order)
    return pl.pallas_call(
        write_out,
        out_shape=(
            jax.ShapeDtypeStruct(updated.shape, F32),
            jax.ShapeDtypeStruct(increment.shape, F32),
        ),
        in_specs=[in_vmem] * 2,
        out_specs=(anywhere, anywhere),
        scratch_shapes=[dma((2,))],
        name="write_out",
    )(
        pltpu.with_memory_space_constraint(updated, pltpu.VMEM),
        pltpu.with_memory_space_constraint(increment, pltpu.VMEM),
    )


def solution(mesh):
    in_specs = (
        P(None, "mem", "lat", None),
        P("mem", None, None, "lat", None),
        P("mem", None, "lat", None),
        P(),
        P(),
        P(),
        P(),
    )
    out_specs = (P("mem", None, "lat", None), P(None, "mem", "lat", None))
    return jax.shard_map(
        on_device, mesh=mesh, in_specs=in_specs, out_specs=out_specs, check_vma=False
    )
```

time: 19.5 us -> 18.4 us (0.944)
  Pallas kernels: 18.7 us -> 17.6 us
    pallas_call x1, Pallas kernels: 17.9 us -> 16.9 us  [on_device(): pl.pallas_call(functools.partial(kernel, n, bands, norm, radius, lev_taps...]
where the time goes in v2:
time: 18.4 us; the launch traced here: 18.3 us
  Pallas kernels  17.6 us (96%)
  between operations  0.64 us (3%)
    pallas_call x1, Pallas kernels, on_device(): pl.pallas_call(functools.partial(kernel, n, bands, norm, radius, lev_taps...  16.9 us
    pallas_call x1, Pallas kernels, on_device(): pl.pallas_call(write_out, out_shape=(jax.ShapeDtypeStruct(updated.shape,...  0.77 us

profile of v2, /device:TPU:1, one launch (start us, length us, event | category | flops | bytes accessed | tf_op | source)
XLA Modules:
  0.0 18.3 jit_solution(1684840612846971164)
XLA Ops:
  0.6 16.9 %step.1 = (f32[4,4,24,256]{3,2,1,0:T(8,128)S(1)}, f32[2,1,24,256]{3,2,1,0:T(8,128)S(1)}) custom-call(f32[2,1,24,256]{3,2,1,0:T(8,128)} %g_hbm.1, bf16[4,2,4,24,256]{4,3,2,1,0:T(8,128)(2,1)} %p_hbm.1, f32[4,4,24,256]{3,2,1,0:T(8,128)} %w_hbm.1, f32[25]{0:T(128)} %lon_hbm.1, f32[25]{0:T(128)} %lat_hbm.1, f32[5]{0:T(128)} %lev_hbm.1, s32[4]{0:T(128)} %order_hbm.1), custom_call_target="tpu_custom_call" | custom-call | tf_op jit(solution)/shard_map/step/pallas_call | solution.py:407
  17.5 0.8 %write_out.1 = (f32[4,4,24,256]{3,2,1,0:T(8,128)}, f32[2,1,24,256]{3,2,1,0:T(8,128)}) custom-call(f32[4,4,24,256]{3,2,1,0:T(8,128)S(1)} %get-tuple-element.4.u_ref, f32[2,1,24,256]{3,2,1,0:T(8,128)S(1)} %get-tuple-element.5.inc_ref), custom_call_target="tpu_custom_call" | custom-call | tf_op jit(solution)/shard_map/write_out/pallas_call | solution.py:452

commit v3 on v2

--- a/solution.py
+++ b/solution.py
@@ -74,7 +74,7 @@
     g_all, p_ref, pf_ref, w_ref, wn_ref, wh_ref, z_ref, zn_ref, acc_ref, f_ref, inc_ref, rs_ref,
     a_hi, a_lo, b_hi, b_lo, k_own, k_halo, k_fwd,
     lon_t, lat_t, lev_t, order,
-    load_sem, known_sem, gs, gr, zs, zr, ws, wr, rsr,
+    pool, known_sem, gr, zr, wr, rsr,
 ):
     me = lax.axis_index("mem")
     band = lax.axis_index("lat")
@@ -86,14 +86,15 @@
     has_low, has_high = band > 0, band < bands - 1
     mesh_ids = pl.DeviceIdType.MESH
 
+    free = list(range(pool.shape[0]))
     loads = [
-        pltpu.make_async_copy(src, dst, load_sem.at[i])
+        pltpu.make_async_copy(src, dst, pool.at[free.pop(0)])
         for i, (src, dst) in enumerate([
             (g_hbm, g_all.at[0]), (w_hbm, w_ref), (lon_hbm, lon_t), (order_hbm, order),
             (p_hbm, p_ref), (lev_hbm, lev_t), (lat_hbm, lat_t),
         ])
     ]
-    load_g, load_w, load_lon, load_order, load_p, load_lev, load_lat = loads
+    g_in, w_in, lon_in, order_in, p_in, lev_in, lat_in = range(len(loads))
     for copy in loads:
         copy.start()
 
@@ -123,72 +124,77 @@
     def source(d):
         return partner(me, d, n) if cube else (me + n - d) % n
 
-    gathers = {
-        d: pltpu.make_async_remote_copy(
-            src_ref=g_all.at[0],
-            dst_ref=g_all.at[d],
-            send_sem=gs.at[d - 1],
-            recv_sem=gr.at[d - 1],
-            device_id=(partner(me, d, n), band),
+    sent = []
+
+    def remote(src, dst, recv_sem, sem, target):
+        return pltpu.make_async_remote_copy(
+            src_ref=src,
+            dst_ref=dst,
+            send_sem=pool.at[sem],
+            recv_sem=recv_sem,
+            device_id=target,
             device_id_type=mesh_ids,
         )
-        for d in range(1, n)
-    }
-
-    def to_bands(low_src, high_src, dst, send_sem, recv_sem):
-        def make(side, src, target):
-            return pltpu.make_async_remote_copy(
-                src_ref=src,
-                dst_ref=dst(side),
-                send_sem=send_sem(side),
-                recv_sem=recv_sem(side),
-                device_id=(me, target),
-                device_id_type=mesh_ids,
-            )
-
-        return make(0, low_src, band + 1), make(1, high_src, band - 1)
-
-    def start(copies):
-        pl.when(has_high)(copies[0].start)
-        pl.when(has_low)(copies[1].start)
-
-    def wait_recv(copies):
-        pl.when(has_low)(copies[0].wait_recv)
-        pl.when(has_high)(copies[1].wait_recv)
-
-    def wait_send(copies):
-        pl.when(has_high)(copies[0].wait_send)
-        pl.when(has_low)(copies[1].wait_send)
-
-    def w_copy(i, size, low, high):
-        at = low - rows + edge, high
+
+    def gather(d):
+        sem = free.pop(0)
+        copy = remote(g_all.at[0], g_all.at[d], gr.at[d - 1], sem, (partner(me, d, n), band))
+        copy.start()
+        sent.append((sem, copy.wait_send))
+        return copy
+
+    odd = band % 2
+    far_then_near = ((1 - odd, band - 1 + 2 * odd), (odd, band + 1 - 2 * odd))
+    both = has_low & has_high
+    one = has_low ^ has_high
+
+    def to_bands(pairs, piece, whole, recv_sem):
+        sem = free.pop(0)
+        for side, target in pairs:
+            @pl.when((target >= 0) & (target < bands))
+            def _():
+                remote(*piece(side), recv_sem, sem, (me, target)).start()
+
+        def wait(semaphore):
+            for count, here in ((2, both), (1, one)):
+                ref = whole(count)
+                pl.when(here)(pltpu.make_async_copy(ref, ref, semaphore).wait)
+
+        sent.append((sem, lambda: wait(pool.at[sem])))
+        return lambda: wait(recv_sem)
+
+    def send_weights(size, low, high, recv_sem):
+        at = ((low, low - rows + edge), (high, high))
         return to_bands(
-            w_ref.at[:, :, low:low + size, :], w_ref.at[:, :, high:high + size, :],
-            lambda s: wn_ref.at[s, :, :, at[s]:at[s] + size, :],
-            lambda s: ws.at[s, i], lambda s: wr.at[s, i],
+            ((0, band + 1), (1, band - 1)),
+            lambda side: (
+                w_ref.at[:, :, at[side][0]:at[side][0] + size, :],
+                wn_ref.at[side, :, :, at[side][1]:at[side][1] + size, :],
+            ),
+            lambda count: wn_ref.at[0:count, :, :, 0:size, :],
+            recv_sem,
         )
 
-    w_copies = [w_copy(0, full, rows - full, 0)]
-    if rem:
-        w_copies.append(w_copy(1, rem, rows - radius, full))
-    z_copies = [
-        to_bands(
-            z_ref.at[q], z_ref.at[q],
-            lambda s, q=q: zn_ref.at[s, q], lambda s, q=q: zs.at[s, q], lambda s, q=q: zr.at[s, q],
-        )
-        for q in range(levels)
-    ]
-
-    load_g.wait()
+    def settle(keep=0):
+        for sem, wait in sent[:len(sent) - keep]:
+            wait()
+            free.append(sem)
+        del sent[:len(sent) - keep]
+
+    def loaded(i):
+        loads[i].wait()
+        free.append(i)
+
+    loaded(g_in)
     neighbours = has_low.astype(jnp.int32) + has_high.astype(jnp.int32)
     pl.semaphore_wait(barrier, len(direct) + neighbours)
     if len(rounds) > 1:
         greet(known_sem.at[0])
-    for d in rounds[0]:
-        gathers[d].start()
-    load_w.wait()
-    for copies in w_copies:
-        start(copies)
+    gathers = {d: gather(d) for d in rounds[0]}
+    loaded(w_in)
+    w_arrival = [send_weights(full, rows - full, 0, wr.at[0])]
+    if rem:
+        w_arrival.append(send_weights(rem, rows - radius, full, wr.at[1]))
 
     row, col = iota((TILE, lons), 0), iota((TILE, lons), 1)
 
@@ -205,25 +211,30 @@
             )
             c_hi[i:i + PACK], c_lo[i:i + PACK] = split(value)
 
-    load_lon.wait()
+    loaded(lon_in)
     lon_matrix(a_hi, a_lo, 1)
-    load_order.wait()
+    loaded(order_in)
     level_of = [
         order[source(q // own_levels) * own_levels + q % own_levels] for q in range(levels)
     ]
-    load_p.wait()
+    loaded(p_in)
 
     def scaled(q):
         for v in range(2):
             for k in range(members):
                 pf_ref[q, v, k * rows:(k + 1) * rows] = p_ref[k, v, level_of[q]].astype(F32) * norm
+
+    z_arrival = {}
 
     def send_level(q):
         d, j = divmod(q, own_levels)
         g0 = jnp.concatenate([g_all[d, 0, j]] * members, axis=0)
         g1 = jnp.concatenate([g_all[d, 1, j]] * members, axis=0)
         z_ref[q] = filter_lon(pf_ref[q, 0] * g0 + pf_ref[q, 1] * g1, a_hi, a_lo)
-        start(z_copies[q])
+        z_arrival[q] = to_bands(
+            far_then_near, lambda side: (z_ref.at[q], zn_ref.at[side, q]),
+            lambda count: zn_ref.at[0:count, q], zr.at[q],
+        )
 
     for j in range(own_levels):
         scaled(j)
@@ -232,8 +243,7 @@
         pl.semaphore_wait(known_sem.at[i - 1], len(direct))
         if i + 1 < len(rounds):
             greet(known_sem.at[i])
-        for d in rounds[i]:
-            gathers[d].start()
+        gathers.update({d: gather(d) for d in rounds[i]})
 
     for q in range(own_levels, levels):
         scaled(q)
@@ -245,7 +255,7 @@
             wn_ref[side] = jnp.zeros(wn_ref.shape[1:], F32)
 
     lon_matrix(b_hi, b_lo, -1)
-    load_lat.wait()
+    loaded(lat_in)
 
     def thirds(shape):
         c, size = iota(shape, 1), shape[1] // 3
@@ -282,7 +292,7 @@
     inside = inside & (c < rows + halo)
     k_fwd[...] = lat_matrix(iota(k_fwd.shape, 0), jnp.where(inside, in_pos, far), third, 1)
 
-    load_lev.wait()
+    loaded(lev_in)
     coef = []
     for l in range(levels):
         coef.append([])
@@ -297,8 +307,8 @@
         for j in range(own_levels):
             send_level(d * own_levels + j)
 
-    for copies in w_copies:
-        wait_recv(copies)
+    for wait in w_arrival:
+        wait()
     s = iota((TILE, lons), 0)
     for k in range(members):
         at = slice(k * rows, (k + 1) * rows)
@@ -315,29 +325,28 @@
             for q in range(levels):
                 total = total + coef[l][q] * own[q]
             acc_ref[k, l] = total
-    for copies in w_copies:
-        wait_send(copies)
-    for copy in gathers.values():
-        copy.wait_send()
 
     ordered = [d * own_levels + j for d in arrival for j in range(own_levels)]
     for q in ordered[:-1]:
-        wait_recv(z_copies[q])
+        z_arrival[q]()
         for k in range(members):
             at = slice(k * rows, (k + 1) * rows)
             y = dot(k_halo[...], stacked(jnp.concatenate([zn_ref[0, q, at], zn_ref[1, q, at]], axis=0)))
             for l in range(levels):
                 acc_ref[k, l] = acc_ref[k, l] + coef[l][q] * y
-        wait_send(z_copies[q])
-
+
+    settle(keep=1)
     q = ordered[-1]
-    wait_recv(z_copies[q])
+    z_arrival[q]()
+    last = []
     for k in range(members):
         at = slice(k * rows, (k + 1) * rows)
-        y = dot(k_halo[...], stacked(jnp.concatenate([zn_ref[0, q, at], zn_ref[1, q, at]], axis=0)))
+        x = jnp.concatenate([zn_ref[0, q, at], zn_ref[1, q, at]], axis=0)
+        last.append(dot(k_halo[...], stacked(x)))
+    for k in range(members):
         for l in range(levels):
             w = jnp.concatenate([w_ref[k, l], wh_ref[k, l]], axis=0)
-            total = acc_ref[k, l] + coef[l][q] * y
+            total = acc_ref[k, l] + coef[l][q] * last[k]
             u = w - STEP_RATE * total / (1.0 + jnp.abs(total))
             u_ref[k, l] = u[0:rows]
             f_ref[k, l] = dot(k_fwd[...], stacked(u))
@@ -352,7 +361,7 @@
                 fields.append(field)
     fields = filter_lon(jnp.concatenate(fields, axis=0), b_hi, b_lo)
 
-    scatters = []
+    scatter_sem = free.pop(0)
     for i, d in enumerate(reversed(arrival)):
         for j in range(own_levels):
             q = d * own_levels + j
@@ -364,25 +373,14 @@
                     inc = inc + terms[k * rows:(k + 1) * rows]
                 inc_ref[d, v, j] = inc
         if d:
-            scatters.append(
-                pltpu.make_async_remote_copy(
-                    src_ref=inc_ref.at[d],
-                    dst_ref=rs_ref.at[d - 1],
-                    send_sem=gs.at[d - 1],
-                    recv_sem=rsr.at[d - 1],
-                    device_id=(source(d), band),
-                    device_id_type=mesh_ids,
-                )
-            )
-            scatters[-1].start()
-    wait_send(z_copies[ordered[-1]])
+            remote(inc_ref.at[d], rs_ref.at[d - 1], rsr, scatter_sem, (source(d), band)).start()
+    settle()
+    pltpu.make_async_copy(rs_ref, rs_ref, rsr).wait()
     result = inc_ref[0]
-    for copy, d in zip(scatters, [d for d in reversed(arrival) if d]):
-        copy.wait_recv()
+    for d in range(1, n):
         result = result + rs_ref[d - 1]
     out_ref[...] = result
-    for copy in scatters:
-        copy.wait_send()
+    pltpu.make_async_copy(rs_ref, rs_ref, pool.at[scatter_sem]).wait()
 
 
 def write_out(u_ref, inc_ref, upd_hbm, inc_hbm, sem):
@@ -436,15 +434,12 @@
             pltpu.SMEM(lat_taps.shape, F32),
             pltpu.SMEM(lev_taps.shape, F32),
             pltpu.SMEM(level_order.shape, jnp.int32),
-            dma((7,)),
+            dma((max(9, n + levels + 1),)),
             pltpu.SemaphoreType.REGULAR((max(1, n.bit_length() - 2),)),
             dma((n - 1,)),
-            dma((n - 1,)),
-            dma((2, levels)),
-            dma((2, levels)),
-            dma((2, 2)),
-            dma((2, 2)),
-            dma((n - 1,)),
+            dma((levels,)),
+            dma((2,)),
+            dma,
         ],
         compiler_params=pltpu.CompilerParams(collective_id=0, has_side_effects=True),
         name="step",

time: 18.4 us -> 18 us (0.978)
  Pallas kernels: 17.6 us -> 17.2 us
    pallas_call x1, Pallas kernels: 16.9 us -> 16.5 us  [on_device(): pl.pallas_call(functools.partial(kernel, n, bands, norm, radius, lev_taps...]
where the time goes in v3:
time: 18 us; the launch traced here: 17.9 us
  Pallas kernels  17.2 us (96%)
  between operations  0.64 us (4%)
    pallas_call x1, Pallas kernels, on_device(): pl.pallas_call(functools.partial(kernel, n, bands, norm, radius, lev_taps...  16.5 us
    pallas_call x1, Pallas kernels, on_device(): pl.pallas_call(write_out, out_shape=(jax.ShapeDtypeStruct(updated.shape,...  0.77 us

profile of v3, /device:TPU:1, one launch (start us, length us, event | category | flops | bytes accessed | tf_op | source)
XLA Modules:
  0.0 17.9 jit_solution(3818104833444993388)
XLA Ops:
  0.6 16.5 %step.1 = (f32[4,4,24,256]{3,2,1,0:T(8,128)S(1)}, f32[2,1,24,256]{3,2,1,0:T(8,128)S(1)}) custom-call(f32[2,1,24,256]{3,2,1,0:T(8,128)} %g_hbm.1, bf16[4,2,4,24,256]{4,3,2,1,0:T(8,128)(2,1)} %p_hbm.1, f32[4,4,24,256]{3,2,1,0:T(8,128)} %w_hbm.1, f32[25]{0:T(128)} %lon_hbm.1, f32[25]{0:T(128)} %lat_hbm.1, f32[5]{0:T(128)} %lev_hbm.1, s32[4]{0:T(128)} %order_hbm.1), custom_call_target="tpu_custom_call" | custom-call | tf_op jit(solution)/shard_map/step/pallas_call | solution.py:405
  17.1 0.8 %write_out.1 = (f32[4,4,24,256]{3,2,1,0:T(8,128)}, f32[2,1,24,256]{3,2,1,0:T(8,128)}) custom-call(f32[4,4,24,256]{3,2,1,0:T(8,128)S(1)} %get-tuple-element.4.u_ref, f32[2,1,24,256]{3,2,1,0:T(8,128)S(1)} %get-tuple-element.5.inc_ref), custom_call_target="tpu_custom_call" | custom-call | tf_op jit(solution)/shard_map/write_out/pallas_call | solution.py:447

commit v4 on v3

--- a/solution.py
+++ b/solution.py
@@ -11,6 +11,7 @@
 STEP_RATE = 0.5
 TILE = 8
 PACK = 16
+PARTS = 2
 F32 = jnp.float32
 BF16 = jnp.bfloat16
 
@@ -225,16 +226,24 @@
                 pf_ref[q, v, k * rows:(k + 1) * rows] = p_ref[k, v, level_of[q]].astype(F32) * norm
 
     z_arrival = {}
+    ordered = [d * own_levels + j for d in arrival for j in range(own_levels)]
+    parts = math.gcd(PARTS, members)
 
     def send_level(q):
         d, j = divmod(q, own_levels)
         g0 = jnp.concatenate([g_all[d, 0, j]] * members, axis=0)
         g1 = jnp.concatenate([g_all[d, 1, j]] * members, axis=0)
         z_ref[q] = filter_lon(pf_ref[q, 0] * g0 + pf_ref[q, 1] * g1, a_hi, a_lo)
-        z_arrival[q] = to_bands(
-            far_then_near, lambda side: (z_ref.at[q], zn_ref.at[side, q]),
-            lambda count: zn_ref.at[0:count, q], zr.at[q],
-        )
+        size = stack // parts if q == ordered[-1] else stack
+        z_arrival[q] = [
+            to_bands(
+                far_then_near,
+                lambda side, at=at: (z_ref.at[q, at:at + size], zn_ref.at[side, q, at:at + size]),
+                lambda count, at=at: zn_ref.at[0:count, q, at:at + size],
+                zr.at[levels + i - 1 if i else q],
+            )
+            for i, at in enumerate(range(0, stack, size))
+        ]
 
     for j in range(own_levels):
         scaled(j)
@@ -326,30 +335,31 @@
                 total = total + coef[l][q] * own[q]
             acc_ref[k, l] = total
 
-    ordered = [d * own_levels + j for d in arrival for j in range(own_levels)]
     for q in ordered[:-1]:
-        z_arrival[q]()
+        z_arrival[q][0]()
         for k in range(members):
             at = slice(k * rows, (k + 1) * rows)
             y = dot(k_halo[...], stacked(jnp.concatenate([zn_ref[0, q, at], zn_ref[1, q, at]], axis=0)))
             for l in range(levels):
                 acc_ref[k, l] = acc_ref[k, l] + coef[l][q] * y
 
-    settle(keep=1)
+    settle(keep=parts)
     q = ordered[-1]
-    z_arrival[q]()
-    last = []
-    for k in range(members):
-        at = slice(k * rows, (k + 1) * rows)
-        x = jnp.concatenate([zn_ref[0, q, at], zn_ref[1, q, at]], axis=0)
-        last.append(dot(k_halo[...], stacked(x)))
-    for k in range(members):
-        for l in range(levels):
-            w = jnp.concatenate([w_ref[k, l], wh_ref[k, l]], axis=0)
-            total = acc_ref[k, l] + coef[l][q] * last[k]
-            u = w - STEP_RATE * total / (1.0 + jnp.abs(total))
-            u_ref[k, l] = u[0:rows]
-            f_ref[k, l] = dot(k_fwd[...], stacked(u))
+    for i in range(parts):
+        z_arrival[q][i]()
+        group = range(i * members // parts, (i + 1) * members // parts)
+        last = {}
+        for k in group:
+            at = slice(k * rows, (k + 1) * rows)
+            x = jnp.concatenate([zn_ref[0, q, at], zn_ref[1, q, at]], axis=0)
+            last[k] = dot(k_halo[...], stacked(x))
+        for k in group:
+            for l in range(levels):
+                w = jnp.concatenate([w_ref[k, l], wh_ref[k, l]], axis=0)
+                total = acc_ref[k, l] + coef[l][q] * last[k]
+                u = w - STEP_RATE * total / (1.0 + jnp.abs(total))
+                u_ref[k, l] = u[0:rows]
+                f_ref[k, l] = dot(k_fwd[...], stacked(u))
 
     fields = []
     for d in reversed(arrival):
@@ -434,10 +444,10 @@
             pltpu.SMEM(lat_taps.shape, F32),
             pltpu.SMEM(lev_taps.shape, F32),
             pltpu.SMEM(level_order.shape, jnp.int32),
-            dma((max(9, n + levels + 1),)),
+            dma((max(9, n + levels + 1) + math.gcd(PARTS, members) - 1,)),
             pltpu.SemaphoreType.REGULAR((max(1, n.bit_length() - 2),)),
             dma((n - 1,)),
-            dma((levels,)),
+            dma((levels + math.gcd(PARTS, members) - 1,)),
             dma((2,)),
             dma,
         ],

time: 18 us -> 17.7 us (0.983)
  Pallas kernels: 17.2 us -> 16.9 us
    pallas_call x1, Pallas kernels: 16.5 us -> 16.2 us  [on_device(): pl.pallas_call(functools.partial(kernel, n, bands, norm, radius, lev_taps...]
where the time goes in v4:
time: 17.7 us; the launch traced here: 17.6 us
  Pallas kernels  16.9 us (95%)
  between operations  0.64 us (4%)
    pallas_call x1, Pallas kernels, on_device(): pl.pallas_call(functools.partial(kernel, n, bands, norm, radius, lev_taps...  16.2 us
    pallas_call x1, Pallas kernels, on_device(): pl.pallas_call(write_out, out_shape=(jax.ShapeDtypeStruct(updated.shape,...  0.77 us

profile of v4, /device:TPU:1, one launch (start us, length us, event | category | flops | bytes accessed | tf_op | source)
XLA Modules:
  0.0 17.6 jit_solution(14073925413814385973)
XLA Ops:
  0.6 16.2 %step.1 = (f32[4,4,24,256]{3,2,1,0:T(8,128)S(1)}, f32[2,1,24,256]{3,2,1,0:T(8,128)S(1)}) custom-call(f32[2,1,24,256]{3,2,1,0:T(8,128)} %g_hbm.1, bf16[4,2,4,24,256]{4,3,2,1,0:T(8,128)(2,1)} %p_hbm.1, f32[4,4,24,256]{3,2,1,0:T(8,128)} %w_hbm.1, f32[25]{0:T(128)} %lon_hbm.1, f32[25]{0:T(128)} %lat_hbm.1, f32[5]{0:T(128)} %lev_hbm.1, s32[4]{0:T(128)} %order_hbm.1), custom_call_target="tpu_custom_call" | custom-call | tf_op jit(solution)/shard_map/step/pallas_call | solution.py:415
  16.8 0.8 %write_out.1 = (f32[4,4,24,256]{3,2,1,0:T(8,128)}, f32[2,1,24,256]{3,2,1,0:T(8,128)}) custom-call(f32[4,4,24,256]{3,2,1,0:T(8,128)S(1)} %get-tuple-element.4.u_ref, f32[2,1,24,256]{3,2,1,0:T(8,128)S(1)} %get-tuple-element.5.inc_ref), custom_call_target="tpu_custom_call" | custom-call | tf_op jit(solution)/shard_map/write_out/pallas_call | solution.py:457

commit v5 on v4

--- a/solution.py
+++ b/solution.py
@@ -72,7 +72,7 @@
     n, bands, norm, radius, lev_width,
     g_hbm, p_hbm, w_hbm, lon_hbm, lat_hbm, lev_hbm, order_hbm,
     u_ref, out_ref,
-    g_all, p_ref, pf_ref, w_ref, wn_ref, wh_ref, z_ref, zn_ref, acc_ref, f_ref, inc_ref, rs_ref,
+    g_all, p_ref, pf_ref, w_ref, wn_ref, wh_ref, x_ref, z_ref, zn_ref, acc_ref, f_ref, inc_ref, rs_ref,
     a_hi, a_lo, b_hi, b_lo, k_own, k_halo, k_fwd,
     lon_t, lat_t, lev_t, order,
     pool, known_sem, gr, zr, wr, rsr,
@@ -228,22 +228,31 @@
     z_arrival = {}
     ordered = [d * own_levels + j for d in arrival for j in range(own_levels)]
     parts = math.gcd(PARTS, members)
+    unfiltered = ordered[own_levels:min(2 * own_levels, levels - 1)]
 
     def send_level(q):
         d, j = divmod(q, own_levels)
         g0 = jnp.concatenate([g_all[d, 0, j]] * members, axis=0)
         g1 = jnp.concatenate([g_all[d, 1, j]] * members, axis=0)
-        z_ref[q] = filter_lon(pf_ref[q, 0] * g0 + pf_ref[q, 1] * g1, a_hi, a_lo)
+        x = pf_ref[q, 0] * g0 + pf_ref[q, 1] * g1
+        src = z_ref.at[q]
+        if q in unfiltered:
+            src = x_ref.at[j]
+            x_ref[j] = x
+        else:
+            z_ref[q] = filter_lon(x, a_hi, a_lo)
         size = stack // parts if q == ordered[-1] else stack
         z_arrival[q] = [
             to_bands(
                 far_then_near,
-                lambda side, at=at: (z_ref.at[q, at:at + size], zn_ref.at[side, q, at:at + size]),
+                lambda side, at=at: (src.at[at:at + size], zn_ref.at[side, q, at:at + size]),
                 lambda count, at=at: zn_ref.at[0:count, q, at:at + size],
                 zr.at[levels + i - 1 if i else q],
             )
             for i, at in enumerate(range(0, stack, size))
         ]
+        if q in unfiltered:
+            z_ref[q] = filter_lon(x, a_hi, a_lo)
 
     for j in range(own_levels):
         scaled(j)
@@ -337,6 +346,9 @@
 
     for q in ordered[:-1]:
         z_arrival[q][0]()
+        if q in unfiltered:
+            z = filter_lon(jnp.concatenate([zn_ref[0, q], zn_ref[1, q]], axis=0), a_hi, a_lo)
+            zn_ref[0, q], zn_ref[1, q] = z[:stack], z[stack:]
         for k in range(members):
             at = slice(k * rows, (k + 1) * rows)
             y = dot(k_halo[...], stacked(jnp.concatenate([zn_ref[0, q, at], zn_ref[1, q, at]], axis=0)))
@@ -361,29 +373,28 @@
                 u_ref[k, l] = u[0:rows]
                 f_ref[k, l] = dot(k_fwd[...], stacked(u))
 
-    fields = []
-    for d in reversed(arrival):
-        for j in range(own_levels):
+    scatter_sem = free.pop(0)
+    backward = arrival[::-1]
+    for group in (backward[:2], backward[2:]):
+        order_q = [d * own_levels + j for d in group for j in range(own_levels)]
+        fields = []
+        for q in order_q:
             for k in range(members):
-                field = coef[0][d * own_levels + j] * f_ref[k, 0]
+                field = coef[0][q] * f_ref[k, 0]
                 for l in range(1, levels):
-                    field = field + coef[l][d * own_levels + j] * f_ref[k, l]
+                    field = field + coef[l][q] * f_ref[k, l]
                 fields.append(field)
-    fields = filter_lon(jnp.concatenate(fields, axis=0), b_hi, b_lo)
-
-    scatter_sem = free.pop(0)
-    for i, d in enumerate(reversed(arrival)):
-        for j in range(own_levels):
-            q = d * own_levels + j
-            at = (i * own_levels + j) * stack
+        fields = filter_lon(jnp.concatenate(fields, axis=0), b_hi, b_lo)
+        for i, q in enumerate(order_q):
             for v in range(2):
-                terms = pf_ref[q, v] * fields[at:at + stack]
+                terms = pf_ref[q, v] * fields[i * stack:(i + 1) * stack]
                 inc = terms[0:rows]
                 for k in range(1, members):
                     inc = inc + terms[k * rows:(k + 1) * rows]
-                inc_ref[d, v, j] = inc
-        if d:
-            remote(inc_ref.at[d], rs_ref.at[d - 1], rsr, scatter_sem, (source(d), band)).start()
+                inc_ref[q // own_levels, v, q % own_levels] = inc
+            d = q // own_levels
+            if d and (q + 1) % own_levels == 0:
+                remote(inc_ref.at[d], rs_ref.at[d - 1], rsr, scatter_sem, (source(d), band)).start()
     settle()
     pltpu.make_async_copy(rs_ref, rs_ref, rsr).wait()
     result = inc_ref[0]
@@ -427,6 +438,7 @@
             vmem(weights.shape, F32),
             vmem((2, members, levels, edge, lons), F32),
             vmem((members, levels, halo, lons), F32),
+            vmem((gradient.shape[1], stack, lons), F32),
             vmem((levels, stack, lons), F32),
             vmem((2, levels, stack, lons), F32),
             vmem((members, levels, rows + halo, lons), F32),

time: 17.7 us -> 17.5 us (0.989)
  Pallas kernels: 16.9 us -> 16.7 us
    pallas_call x1, Pallas kernels: 16.2 us -> 15.9 us  [on_device(): pl.pallas_call(functools.partial(kernel, n, bands, norm, radius, lev_taps...]
where the time goes in v5:
time: 17.5 us; the launch traced here: 17.3 us
  Pallas kernels  16.7 us (95%)
  between operations  0.64 us (4%)
    pallas_call x1, Pallas kernels, on_device(): pl.pallas_call(functools.partial(kernel, n, bands, norm, radius, lev_taps...  15.9 us
    pallas_call x1, Pallas kernels, on_device(): pl.pallas_call(write_out, out_shape=(jax.ShapeDtypeStruct(updated.shape,...  0.77 us

profile of v5, /device:TPU:1, one launch (start us, length us, event | category | flops | bytes accessed | tf_op | source)
XLA Modules:
  0.0 17.3 jit_solution(12928808616239069481)
XLA Ops:
  0.6 15.9 %step.1 = (f32[4,4,24,256]{3,2,1,0:T(8,128)S(1)}, f32[2,1,24,256]{3,2,1,0:T(8,128)S(1)}) custom-call(f32[2,1,24,256]{3,2,1,0:T(8,128)} %g_hbm.1, bf16[4,2,4,24,256]{4,3,2,1,0:T(8,128)(2,1)} %p_hbm.1, f32[4,4,24,256]{3,2,1,0:T(8,128)} %w_hbm.1, f32[25]{0:T(128)} %lon_hbm.1, f32[25]{0:T(128)} %lat_hbm.1, f32[5]{0:T(128)} %lev_hbm.1, s32[4]{0:T(128)} %order_hbm.1), custom_call_target="tpu_custom_call" | custom-call | tf_op jit(solution)/shard_map/step/pallas_call | solution.py:426
  16.5 0.8 %write_out.1 = (f32[4,4,24,256]{3,2,1,0:T(8,128)}, f32[2,1,24,256]{3,2,1,0:T(8,128)}) custom-call(f32[4,4,24,256]{3,2,1,0:T(8,128)S(1)} %get-tuple-element.4.u_ref, f32[2,1,24,256]{3,2,1,0:T(8,128)S(1)} %get-tuple-element.5.inc_ref), custom_call_target="tpu_custom_call" | custom-call | tf_op jit(solution)/shard_map/write_out/pallas_call | solution.py:469

commit v6 on v5

--- a/solution.py
+++ b/solution.py
@@ -91,11 +91,11 @@
     loads = [
         pltpu.make_async_copy(src, dst, pool.at[free.pop(0)])
         for i, (src, dst) in enumerate([
-            (g_hbm, g_all.at[0]), (w_hbm, w_ref), (lon_hbm, lon_t), (order_hbm, order),
+            (g_hbm, g_all.at[0]), (lon_hbm, lon_t), (order_hbm, order), (w_hbm, w_ref),
             (p_hbm, p_ref), (lev_hbm, lev_t), (lat_hbm, lat_t),
         ])
     ]
-    g_in, w_in, lon_in, order_in, p_in, lev_in, lat_in = range(len(loads))
+    g_in, lon_in, order_in, w_in, p_in, lev_in, lat_in = range(len(loads))
     for copy in loads:
         copy.start()
 
@@ -145,14 +145,14 @@
         return copy
 
     odd = band % 2
-    far_then_near = ((1 - odd, band - 1 + 2 * odd), (odd, band + 1 - 2 * odd))
+    far_then_near = ((1 - odd, band - 1 + 2 * odd, True), (odd, band + 1 - 2 * odd, True))
     both = has_low & has_high
     one = has_low ^ has_high
 
     def to_bands(pairs, piece, whole, recv_sem):
         sem = free.pop(0)
-        for side, target in pairs:
-            @pl.when((target >= 0) & (target < bands))
+        for side, target, here in pairs:
+            @pl.when((target >= 0) & (target < bands) & here)
             def _():
                 remote(*piece(side), recv_sem, sem, (me, target)).start()
 
@@ -167,7 +167,7 @@
     def send_weights(size, low, high, recv_sem):
         at = ((low, low - rows + edge), (high, high))
         return to_bands(
-            ((0, band + 1), (1, band - 1)),
+            ((1, band - 1, odd == 0), (0, band + 1, True), (1, band - 1, odd == 1)),
             lambda side: (
                 w_ref.at[:, :, at[side][0]:at[side][0] + size, :],
                 wn_ref.at[side, :, :, at[side][1]:at[side][1] + size, :],
@@ -187,6 +187,8 @@
         free.append(i)
 
     loaded(g_in)
+    loaded(lon_in)
+    loaded(order_in)
     neighbours = has_low.astype(jnp.int32) + has_high.astype(jnp.int32)
     pl.semaphore_wait(barrier, len(direct) + neighbours)
     if len(rounds) > 1:
@@ -212,9 +214,7 @@
             )
             c_hi[i:i + PACK], c_lo[i:i + PACK] = split(value)
 
-    loaded(lon_in)
     lon_matrix(a_hi, a_lo, 1)
-    loaded(order_in)
     level_of = [
         order[source(q // own_levels) * own_levels + q % own_levels] for q in range(levels)
     ]
@@ -254,9 +254,12 @@
         if q in unfiltered:
             z_ref[q] = filter_lon(x, a_hi, a_lo)
 
+    early = len(sent)
     for j in range(own_levels):
         scaled(j)
         send_level(j)
+    loaded(lev_in)
+    loaded(lat_in)
     for i in range(1, len(rounds)):
         pl.semaphore_wait(known_sem.at[i - 1], len(direct))
         if i + 1 < len(rounds):
@@ -273,7 +276,6 @@
             wn_ref[side] = jnp.zeros(wn_ref.shape[1:], F32)
 
     lon_matrix(b_hi, b_lo, -1)
-    loaded(lat_in)
 
     def thirds(shape):
         c, size = iota(shape, 1), shape[1] // 3
@@ -310,7 +312,6 @@
     inside = inside & (c < rows + halo)
     k_fwd[...] = lat_matrix(iota(k_fwd.shape, 0), jnp.where(inside, in_pos, far), third, 1)
 
-    loaded(lev_in)
     coef = []
     for l in range(levels):
         coef.append([])
@@ -321,6 +322,8 @@
             coef[l].append(jnp.where(inside, value, 0.0))
 
     for d in arrival[1:]:
+        if d == arrival[2]:
+            settle(keep=len(sent) - early)
         gathers[d].wait_recv()
         for j in range(own_levels):
             send_level(d * own_levels + j)
@@ -375,7 +378,7 @@
 
     scatter_sem = free.pop(0)
     backward = arrival[::-1]
-    for group in (backward[:2], backward[2:]):
+    for group in (backward[0:3], backward[3:]):
         order_q = [d * own_levels + j for d in group for j in range(own_levels)]
         fields = []
         for q in order_q:
@@ -456,7 +459,7 @@
             pltpu.SMEM(lat_taps.shape, F32),
             pltpu.SMEM(lev_taps.shape, F32),
             pltpu.SMEM(level_order.shape, jnp.int32),
-            dma((max(9, n + levels + 1) + math.gcd(PARTS, members) - 1,)),
+            dma((max(7, n + levels - 1),)),
             pltpu.SemaphoreType.REGULAR((max(1, n.bit_length() - 2),)),
             dma((n - 1,)),
             dma((levels + math.gcd(PARTS, members) - 1,)),

time: 17.5 us -> 17.5 us (level)
  no operation moved by 1% of the time
where the time goes in v6:
time: 17.5 us; the launch traced here: 17.3 us
  Pallas kernels  16.7 us (95%)
  between operations  0.64 us (4%)
    pallas_call x1, Pallas kernels, on_device(): pl.pallas_call(functools.partial(kernel, n, bands, norm, radius, lev_taps...  15.9 us
    pallas_call x1, Pallas kernels, on_device(): pl.pallas_call(write_out, out_shape=(jax.ShapeDtypeStruct(updated.shape,...  0.77 us

profile of v6, /device:TPU:1, one launch (start us, length us, event | category | flops | bytes accessed | tf_op | source)
XLA Modules:
  0.0 17.3 jit_solution(17401309938079733990)
XLA Ops:
  0.6 15.9 %step.1 = (f32[4,4,24,256]{3,2,1,0:T(8,128)S(1)}, f32[2,1,24,256]{3,2,1,0:T(8,128)S(1)}) custom-call(f32[2,1,24,256]{3,2,1,0:T(8,128)} %g_hbm.1, bf16[4,2,4,24,256]{4,3,2,1,0:T(8,128)(2,1)} %p_hbm.1, f32[4,4,24,256]{3,2,1,0:T(8,128)} %w_hbm.1, f32[25]{0:T(128)} %lon_hbm.1, f32[25]{0:T(128)} %lat_hbm.1, f32[5]{0:T(128)} %lev_hbm.1, s32[4]{0:T(128)} %order_hbm.1), custom_call_target="tpu_custom_call" | custom-call | tf_op jit(solution)/shard_map/step/pallas_call | solution.py:429
  16.6 0.8 %write_out.1 = (f32[4,4,24,256]{3,2,1,0:T(8,128)}, f32[2,1,24,256]{3,2,1,0:T(8,128)}) custom-call(f32[4,4,24,256]{3,2,1,0:T(8,128)S(1)} %get-tuple-element.4.u_ref, f32[2,1,24,256]{3,2,1,0:T(8,128)S(1)} %get-tuple-element.5.inc_ref), custom_call_target="tpu_custom_call" | custom-call | tf_op jit(solution)/shard_map/write_out/pallas_call | solution.py:472

commit v7 on v6

--- a/solution.py
+++ b/solution.py
@@ -36,10 +36,14 @@
     return lax.dot_general(a, b, (((1,), (0,)), ((), ())), preferred_element_type=F32)
 
 
+def filter_split(high, low, c_hi, c_lo):
+    size = high.shape[0]
+    both = dot(jnp.concatenate([high, low], axis=0), c_hi[...])
+    return both[:size] + (both[size:] + dot(high, c_lo[...]))
+
+
 def filter_lon(x, c_hi, c_lo):
-    high, low = split(x)
-    both = dot(jnp.concatenate([high, low], axis=0), c_hi[...])
-    return both[:x.shape[0]] + (both[x.shape[0]:] + dot(high, c_lo[...]))
+    return filter_split(*split(x), c_hi, c_lo)
 
 
 def packed(rows):
@@ -72,7 +76,7 @@
     n, bands, norm, radius, lev_width,
     g_hbm, p_hbm, w_hbm, lon_hbm, lat_hbm, lev_hbm, order_hbm,
     u_ref, out_ref,
-    g_all, p_ref, pf_ref, w_ref, wn_ref, wh_ref, x_ref, z_ref, zn_ref, acc_ref, f_ref, inc_ref, rs_ref,
+    g_all, p_ref, pf_ref, w_ref, wn_ref, wh_ref, x_ref, z_ref, zn_ref, acc_ref, f_hi, f_lo, inc_ref, rs_ref,
     a_hi, a_lo, b_hi, b_lo, k_own, k_halo, k_fwd,
     lon_t, lat_t, lev_t, order,
     pool, known_sem, gr, zr, wr, rsr,
@@ -360,6 +364,16 @@
 
     settle(keep=parts)
     q = ordered[-1]
+    backward = arrival[::-1]
+    outgoing = [d * own_levels + j for d in backward[:-1] for j in range(own_levels)]
+    part = stack // parts
+
+    def filtered_part(g):
+        at = slice(g * part, (g + 1) * part)
+        high = jnp.concatenate([f_hi[j, at] for j in outgoing], axis=0)
+        low = jnp.concatenate([f_lo[j, at] for j in outgoing], axis=0)
+        return filter_split(high, low, b_hi, b_lo)
+
     for i in range(parts):
         z_arrival[q][i]()
         group = range(i * members // parts, (i + 1) * members // parts)
@@ -368,36 +382,46 @@
             at = slice(k * rows, (k + 1) * rows)
             x = jnp.concatenate([zn_ref[0, q, at], zn_ref[1, q, at]], axis=0)
             last[k] = dot(k_halo[...], stacked(x))
+        if i == parts - 1:
+            filtered = [filtered_part(g) for g in range(i)]
+        fields = {j: [] for j in range(levels)}
         for k in group:
+            y = []
             for l in range(levels):
                 w = jnp.concatenate([w_ref[k, l], wh_ref[k, l]], axis=0)
                 total = acc_ref[k, l] + coef[l][q] * last[k]
                 u = w - STEP_RATE * total / (1.0 + jnp.abs(total))
                 u_ref[k, l] = u[0:rows]
-                f_ref[k, l] = dot(k_fwd[...], stacked(u))
+                y.append(dot(k_fwd[...], stacked(u)))
+            for j in range(levels):
+                field = coef[0][j] * y[0]
+                for l in range(1, levels):
+                    field = field + coef[l][j] * y[l]
+                fields[j].append(field)
+        at = slice(group[0] * rows, (group[-1] + 1) * rows)
+        for j in range(levels):
+            f_hi[j, at], f_lo[j, at] = split(jnp.concatenate(fields[j], axis=0))
 
     scatter_sem = free.pop(0)
-    backward = arrival[::-1]
-    for group in (backward[0:3], backward[3:]):
-        order_q = [d * own_levels + j for d in group for j in range(own_levels)]
-        fields = []
-        for q in order_q:
-            for k in range(members):
-                field = coef[0][q] * f_ref[k, 0]
-                for l in range(1, levels):
-                    field = field + coef[l][q] * f_ref[k, l]
-                fields.append(field)
-        fields = filter_lon(jnp.concatenate(fields, axis=0), b_hi, b_lo)
-        for i, q in enumerate(order_q):
-            for v in range(2):
-                terms = pf_ref[q, v] * fields[i * stack:(i + 1) * stack]
-                inc = terms[0:rows]
-                for k in range(1, members):
-                    inc = inc + terms[k * rows:(k + 1) * rows]
-                inc_ref[q // own_levels, v, q % own_levels] = inc
-            d = q // own_levels
-            if d and (q + 1) % own_levels == 0:
-                remote(inc_ref.at[d], rs_ref.at[d - 1], rsr, scatter_sem, (source(d), band)).start()
+    filtered.append(filtered_part(parts - 1))
+
+    def increment(q, fields):
+        for v in range(2):
+            inc = None
+            for g, field in enumerate(fields):
+                terms = pf_ref[q, v, g * field.shape[0]:(g + 1) * field.shape[0]] * field
+                for k in range(0, field.shape[0], rows):
+                    term = terms[k:k + rows]
+                    inc = term if inc is None else inc + term
+            inc_ref[q // own_levels, v, q % own_levels] = inc
+
+    for i, q in enumerate(outgoing):
+        increment(q, [f[i * part:(i + 1) * part] for f in filtered])
+        d = q // own_levels
+        if (q + 1) % own_levels == 0:
+            remote(inc_ref.at[d], rs_ref.at[d - 1], rsr, scatter_sem, (source(d), band)).start()
+    for q in range(own_levels):
+        increment(q, [filter_split(f_hi[q], f_lo[q], b_hi, b_lo)])
     settle()
     pltpu.make_async_copy(rs_ref, rs_ref, rsr).wait()
     result = inc_ref[0]
@@ -445,7 +469,8 @@
             vmem((levels, stack, lons), F32),
             vmem((2, levels, stack, lons), F32),
             vmem((members, levels, rows + halo, lons), F32),
-            vmem(weights.shape, F32),
+            vmem((levels, stack, lons), BF16),
+            vmem((levels, stack, lons), BF16),
             vmem((n,) + gradient.shape, F32),
             vmem((n - 1,) + gradient.shape, F32),
             vmem((lons, lons), BF16),

time: 17.5 us -> 17.5 us (level)
  no operation moved by 1% of the time
where the time goes in v7:
time: 17.5 us; the launch traced here: 17.3 us
  Pallas kernels  16.7 us (95%)
  between operations  0.64 us (4%)
    pallas_call x1, Pallas kernels, on_device(): pl.pallas_call(functools.partial(kernel, n, bands, norm, radius, lev_taps...  15.9 us
    pallas_call x1, Pallas kernels, on_device(): pl.pallas_call(write_out, out_shape=(jax.ShapeDtypeStruct(updated.shape,...  0.77 us

profile of v7, /device:TPU:1, one launch (start us, length us, event | category | flops | bytes accessed | tf_op | source)
XLA Modules:
  0.0 17.3 jit_solution(2477763407734566979)
XLA Ops:
  0.6 15.9 %step.1 = (f32[4,4,24,256]{3,2,1,0:T(8,128)S(1)}, f32[2,1,24,256]{3,2,1,0:T(8,128)S(1)}) custom-call(f32[2,1,24,256]{3,2,1,0:T(8,128)} %g_hbm.1, bf16[4,2,4,24,256]{4,3,2,1,0:T(8,128)(2,1)} %p_hbm.1, f32[4,4,24,256]{3,2,1,0:T(8,128)} %w_hbm.1, f32[25]{0:T(128)} %lon_hbm.1, f32[25]{0:T(128)} %lat_hbm.1, f32[5]{0:T(128)} %lev_hbm.1, s32[4]{0:T(128)} %order_hbm.1), custom_call_target="tpu_custom_call" | custom-call | tf_op jit(solution)/shard_map/step/pallas_call | solution.py:453
  16.6 0.8 %write_out.1 = (f32[4,4,24,256]{3,2,1,0:T(8,128)}, f32[2,1,24,256]{3,2,1,0:T(8,128)}) custom-call(f32[4,4,24,256]{3,2,1,0:T(8,128)S(1)} %get-tuple-element.4.u_ref, f32[2,1,24,256]{3,2,1,0:T(8,128)S(1)} %get-tuple-element.5.inc_ref), custom_call_target="tpu_custom_call" | custom-call | tf_op jit(solution)/shard_map/write_out/pallas_call | solution.py:497

commit v8 on v7

--- a/solution.py
+++ b/solution.py
@@ -100,8 +100,7 @@
         ])
     ]
     g_in, lon_in, order_in, w_in, p_in, lev_in, lat_in = range(len(loads))
-    for copy in loads:
-        copy.start()
+    loads[g_in].start()
 
     barrier = pltpu.get_barrier_semaphore()
     cube = not n & (n - 1)
@@ -125,6 +124,9 @@
     @pl.when(has_high)
     def _():
         pl.semaphore_signal(barrier, inc=1, device_id=(me, band + 1), device_id_type=mesh_ids)
+
+    for copy in loads[1:]:
+        copy.start()
 
     def source(d):
         return partner(me, d, n) if cube else (me + n - d) % n

time: 17.5 us -> 17.5 us (level)
  no operation moved by 1% of the time
where the time goes in v8:
time: 17.5 us; the launch traced here: 17.3 us
  Pallas kernels  16.7 us (95%)
  between operations  0.64 us (4%)
    pallas_call x1, Pallas kernels, on_device(): pl.pallas_call(functools.partial(kernel, n, bands, norm, radius, lev_taps...  15.9 us
    pallas_call x1, Pallas kernels, on_device(): pl.pallas_call(write_out, out_shape=(jax.ShapeDtypeStruct(updated.shape,...  0.77 us

profile of v8, /device:TPU:1, one launch (start us, length us, event | category | flops | bytes accessed | tf_op | source)
XLA Modules:
  0.0 17.3 jit_solution(7970560080211635003)
XLA Ops:
  0.6 15.9 %step.1 = (f32[4,4,24,256]{3,2,1,0:T(8,128)S(1)}, f32[2,1,24,256]{3,2,1,0:T(8,128)S(1)}) custom-call(f32[2,1,24,256]{3,2,1,0:T(8,128)} %g_hbm.1, bf16[4,2,4,24,256]{4,3,2,1,0:T(8,128)(2,1)} %p_hbm.1, f32[4,4,24,256]{3,2,1,0:T(8,128)} %w_hbm.1, f32[25]{0:T(128)} %lon_hbm.1, f32[25]{0:T(128)} %lat_hbm.1, f32[5]{0:T(128)} %lev_hbm.1, s32[4]{0:T(128)} %order_hbm.1), custom_call_target="tpu_custom_call" | custom-call | tf_op jit(solution)/shard_map/step/pallas_call | solution.py:455
  16.6 0.8 %write_out.1 = (f32[4,4,24,256]{3,2,1,0:T(8,128)}, f32[2,1,24,256]{3,2,1,0:T(8,128)}) custom-call(f32[4,4,24,256]{3,2,1,0:T(8,128)S(1)} %get-tuple-element.4.u_ref, f32[2,1,24,256]{3,2,1,0:T(8,128)S(1)} %get-tuple-element.5.inc_ref), custom_call_target="tpu_custom_call" | custom-call | tf_op jit(solution)/shard_map/write_out/pallas_call | solution.py:499

commit v9 on v7

--- a/solution.py
+++ b/solution.py
@@ -195,9 +195,9 @@
     loaded(order_in)
     neighbours = has_low.astype(jnp.int32) + has_high.astype(jnp.int32)
     pl.semaphore_wait(barrier, len(direct) + neighbours)
+    gathers = {d: gather(d) for d in rounds[0]}
     if len(rounds) > 1:
         greet(known_sem.at[0])
-    gathers = {d: gather(d) for d in rounds[0]}
     loaded(w_in)
     w_arrival = [send_weights(full, rows - full, 0, wr.at[0])]
     if rem:

time: 17.5 us -> 17.5 us (level)
  no operation moved by 1% of the time
where the time goes in v9:
time: 17.5 us; the launch traced here: 17.3 us
  Pallas kernels  16.7 us (95%)
  between operations  0.64 us (4%)
    pallas_call x1, Pallas kernels, on_device(): pl.pallas_call(functools.partial(kernel, n, bands, norm, radius, lev_taps...  15.9 us
    pallas_call x1, Pallas kernels, on_device(): pl.pallas_call(write_out, out_shape=(jax.ShapeDtypeStruct(updated.shape,...  0.77 us

profile of v9, /device:TPU:1, one launch (start us, length us, event | category | flops | bytes accessed | tf_op | source)
XLA Modules:
  0.0 17.3 jit_solution(17161655925809091093)
XLA Ops:
  0.6 15.9 %step.1 = (f32[4,4,24,256]{3,2,1,0:T(8,128)S(1)}, f32[2,1,24,256]{3,2,1,0:T(8,128)S(1)}) custom-call(f32[2,1,24,256]{3,2,1,0:T(8,128)} %g_hbm.1, bf16[4,2,4,24,256]{4,3,2,1,0:T(8,128)(2,1)} %p_hbm.1, f32[4,4,24,256]{3,2,1,0:T(8,128)} %w_hbm.1, f32[25]{0:T(128)} %lon_hbm.1, f32[25]{0:T(128)} %lat_hbm.1, f32[5]{0:T(128)} %lev_hbm.1, s32[4]{0:T(128)} %order_hbm.1), custom_call_target="tpu_custom_call" | custom-call | tf_op jit(solution)/shard_map/step/pallas_call | solution.py:453
  16.5 0.8 %write_out.1 = (f32[4,4,24,256]{3,2,1,0:T(8,128)}, f32[2,1,24,256]{3,2,1,0:T(8,128)}) custom-call(f32[4,4,24,256]{3,2,1,0:T(8,128)S(1)} %get-tuple-element.4.u_ref, f32[2,1,24,256]{3,2,1,0:T(8,128)S(1)} %get-tuple-element.5.inc_ref), custom_call_target="tpu_custom_call" | custom-call | tf_op jit(solution)/shard_map/write_out/pallas_call | solution.py:497
